TPU v7x, 256 devices: a whole 4x4x8 slice. The times are simulated.
256 devices in a mesh: ctx: 32 (over z, y_hi, core), tp: 8 (over x, y_lo).
Axes of the slice: x: 4, y: 4 (y_hi: 2, y_lo: 2; y = y_hi * 2 + y_lo), z: 8, core: 2. Of those that a mesh axis runs over, the one named last changes fastest.
Arguments:
- queries: bfloat16 [64, 2, 8192], P('ctx', None, 'tp'), may hold values from -60 to 60
- new_keys: bfloat16 [2, 64, 1024], P(None, 'ctx', 'tp'), may hold values from -9.5625 to 9.5625
- new_values: bfloat16 [2, 64, 1024], P(None, 'ctx', 'tp'), may hold values from -6 to 6
- cache_keys: bfloat16 [2, 131072, 1024], P(None, 'ctx', 'tp'), may hold values from -6 to 6
- cache_values: bfloat16 [2, 131072, 1024], P(None, 'ctx', 'tp'), may hold values from -6 to 6
- hist_len: int32 [2], replicated, may hold values from 32768 to 122880, as said below
- page_owner: int32 [2, 32], replicated, may hold values from 0 to 31, as said below
- out_weight: bfloat16 [8192, 8192], P('tp', 'ctx'), may hold values from -0.0625 to 0.0625
Outputs:
- attended: bfloat16 [64, 2, 8192], P('tp', None, 'ctx')
- stored_keys: bfloat16 [32, 2, 2, 1024], P('ctx', None, None, 'tp')
- stored_values: bfloat16 [32, 2, 2, 1024], P('ctx', None, None, 'tp')
Inputs may be any that keep to these rules, and one draw needn't show every extreme that they name: `hist_len`: some request has the full length. `page_owner`: each row lists every device once; page b of request r holds its new-turn tokens b * 2 to (b + 1) * 2 - 1; some column b holds one value in every row.
All inputs are finite; a program needn't handle non-finite values.
Results may differ from a plain program's by a relative error of at most 0.0085.
Values may be sent and summed in bfloat16 or wider, within the bound.
A program may use at most 64 MiB of HBM per device.

v0:
```python
import math

import jax
import jax.numpy as jnp
from jax import lax
from jax.sharding import PartitionSpec as P

HD = 128


FLOOR_SCORE = -1e30


def in_one_piece(arrays, axis, split_dim, concat_dim, along):
    widths = [a.shape[along] for a in arrays]
    both = jnp.concatenate(arrays, axis=along)
    filled = lax.all_to_all(both, axis, split_axis=split_dim, concat_axis=concat_dim, tiled=True)
    return tuple(jnp.split(filled, [sum(widths[:k]) for k in range(1, len(widths))], axis=along))


def copy_for_each(array, axis):
    size = lax.axis_size(axis)
    return lax.all_to_all(
        jnp.broadcast_to(array[None], (size, *array.shape)), axis, 0, 0, tiled=True
    )


def joined_along(parts, dim):
    dims = list(parts.shape[1:])
    dims[dim] *= parts.shape[0]
    return jnp.moveaxis(parts, 0, dim).reshape(dims)


def gathered_copies(array, axis, dim):
    parts = copy_for_each(array, axis)
    return joined_along(parts, dim)


def over_copies(array, axis):
    return copy_for_each(array, axis).max(axis=0)


def of_everyone(array, axis):
    everything = copy_for_each(array, axis)
    return jnp.sum(everything, axis=0)


def cut_along(array, dim, size):
    dims = array.shape
    parts = array.reshape(*dims[:dim], size, dims[dim] // size, *dims[dim + 1 :])
    return jnp.moveaxis(parts, dim, 0)


def sum_at_owner(array, axis, dim):
    size = lax.axis_size(axis)
    parts = lax.all_to_all(cut_along(array, dim, size), axis, 0, 0, tiled=True)
    return jnp.sum(parts, axis=0)


def online_step(progress, scores, value_block, visible):
    accumulated, peak_score, running_total = progress
    masked = jnp.where(visible, scores, FLOOR_SCORE)
    new_peak = jnp.maximum(peak_score, jnp.max(masked, axis=-1))
    shrink = jnp.exp(peak_score - new_peak)
    weights = jnp.where(visible, jnp.exp(masked - new_peak[..., None]), 0.0)
    running_total = running_total * shrink + jnp.sum(weights, axis=-1)
    update = jnp.einsum(
        "nrkgb,rbkd->nrkgd",
        weights.astype(jnp.bfloat16),
        value_block,
        preferred_element_type=jnp.float32,
    )
    accumulated = accumulated * shrink[..., None] + update
    return (accumulated, new_peak, running_total)


def on_device(
    queries, new_keys, new_values, cache_keys, cache_values, hist_len, page_owner, out_weight
):
    members = lax.axis_size("ctx")
    own_index = lax.axis_index("ctx")
    requests, page_rows, kv_width = new_keys.shape
    heads_width = queries.shape[2]
    head_size = HD
    kv_heads = kv_width // head_size
    group_size = heads_width // kv_width
    history = cache_keys.shape[1]
    half_size = history // 2
    turn_total = page_rows * members
    key_block = min(512, half_size)
    block_count = history // key_block
    score_scale = 1.0 / math.sqrt(head_size)
    owner_row = lax.dynamic_index_in_dim(page_owner, own_index, 1, keepdims=False)
    device_ids = jnp.arange(members, dtype=jnp.int32)
    targets = (owner_row[None, :] == device_ids[:, None]).astype(jnp.bfloat16)
    send_keys = targets[:, :, None, None] * new_keys[None]
    send_values = targets[:, :, None, None] * new_values[None]
    got_keys, got_values = in_one_piece((send_keys, send_values), "ctx", 0, 0, 1)
    own_keys = jnp.sum(got_keys, axis=0)
    own_values = jnp.sum(got_values, axis=0)
    mine_mask = (page_owner == own_index).astype(jnp.int32)
    anchor = jnp.sum(mine_mask * device_ids[None, :], axis=1)
    key_turn = anchor[:, None] * page_rows + jnp.arange(page_rows, dtype=jnp.int32)[None, :]
    own_keys4 = own_keys.reshape(requests, page_rows, kv_heads, head_size)
    own_values4 = own_values.reshape(requests, page_rows, kv_heads, head_size)
    local_slot = jnp.arange(history, dtype=jnp.int32)
    position = jnp.where(
        local_slot < half_size,
        own_index * half_size + local_slot,
        (2 * members - 1 - own_index) * half_size + local_slot - half_size,
    )
    alive_slot = position[None, :] < hist_len[:, None]
    query_piece = gathered_copies(queries, "ctx", 0)
    row_count = query_piece.shape[0]
    grouped = query_piece.reshape(row_count, requests, kv_heads, group_size, head_size)
    start_state = (
        jnp.zeros((row_count, requests, kv_heads, group_size, head_size), jnp.float32),
        jnp.full((row_count, requests, kv_heads, group_size), FLOOR_SCORE, jnp.float32),
        jnp.zeros((row_count, requests, kv_heads, group_size), jnp.float32),
    )

    def visit(step_index, progress):
        offset = step_index * key_block
        key_slab = lax.dynamic_slice_in_dim(cache_keys, offset, key_block, 1).reshape(
            requests, key_block, kv_heads, head_size
        )
        value_slab = lax.dynamic_slice_in_dim(cache_values, offset, key_block, 1).reshape(
            requests, key_block, kv_heads, head_size
        )
        live_slab = lax.dynamic_slice_in_dim(alive_slot, offset, key_block, 1)
        scores = (
            jnp.einsum("nrkgd,rbkd->nrkgb", grouped, key_slab, preferred_element_type=jnp.float32)
            * score_scale
        )
        return online_step(progress, scores, value_slab, live_slab[None, :, None, None, :])

    progress = lax.fori_loop(0, block_count, visit, start_state)
    query_turn = jnp.arange(row_count, dtype=jnp.int32)
    scores = (
        jnp.einsum("nrkgd,rbkd->nrkgb", grouped, own_keys4, preferred_element_type=jnp.float32)
        * score_scale
    )
    visible = (key_turn[None, :, :] <= query_turn[:, None, None])[:, :, None, None, :]
    progress = online_step(progress, scores, own_values4, visible)
    accumulated, peak_score, running_total = tuple((piece for piece in progress))
    global_peak = over_copies(peak_score, "ctx")
    weight = jnp.exp(peak_score - global_peak)
    global_total = of_everyone(running_total * weight, "ctx")
    shared_rows = sum_at_owner(accumulated * (weight / global_total)[..., None], "ctx", 0)
    attention = gathered_copies(shared_rows.astype(jnp.bfloat16), "ctx", 0)
    flattened = attention.reshape(turn_total, requests, heads_width)
    attended = sum_at_owner(
        jnp.einsum("trc,cd->trd", flattened, out_weight, preferred_element_type=jnp.float32),
        "tp",
        0,
    ).astype(jnp.bfloat16)
    return (attended, own_keys[None], own_values[None])


def solution(mesh):
    return jax.shard_map(
        on_device,
        mesh=mesh,
        in_specs=(
            P("ctx", None, "tp"),
            P(None, "ctx", "tp"),
            P(None, "ctx", "tp"),
            P(None, "ctx", "tp"),
            P(None, "ctx", "tp"),
            P(),
            P(),
            P("tp", "ctx"),
        ),
        out_specs=(P("tp", None, "ctx"), P("ctx", None, None, "tp"), P("ctx", None, None, "tp")),
        check_vma=False,
    )
```

profile of v0, /device:TPU:1, one launch (start us, length us, event | category | flops | bytes accessed | tf_op | source)
XLA Modules:
  0.0 168.1 jit_solution(14042479118878672945)
XLA Ops:
  0.6 0.9 dynamic-slice_reduce_fusion
  3.1 12.7 %all-to-all-start.1 = ((bf16[32,4,2,128]{3,2,1,0:T(2,128)(2,1)}), bf16[32,4,2,128]{3,2,1,0:T(2,128)(2,1)S(1)}, u32[]{:S(2)}, u32[]{:S(2)}) async-start(bf16[32,4,2,128]{3,2,1,0:T(2,128)(2,1)} %pad_maximum_fusion), calls=%async_computation.1 | async-start | bytes 131072 | tf_op jit(solution)/shard_map/all_to_all | solution.py:17
  17.5 8.2 %all-to-all-done.1 = bf16[32,4,2,128]{3,2,1,0:T(2,128)(2,1)S(1)} async-done(((bf16[32,4,2,128]{3,2,1,0:T(2,128)(2,1)}), bf16[32,4,2,128]{3,2,1,0:T(2,128)(2,1)S(1)}, u32[]{:S(2)}, u32[]{:S(2)}) %all-to-all-start.1) | async-done | bytes 65568 | tf_op jit(solution)/shard_map/all_to_all | solution.py:17
  25.7 1.5 broadcast_in_dim.124
  27.2 3.9 %all-to-all-start = ((bf16[32,2,2,1024]{3,2,1,0:T(2,128)(2,1)}), bf16[32,2,2,1024]{3,2,1,0:T(2,128)(2,1)S(1)}, u32[]{:S(2)}, u32[]{:S(2)}) async-start(bf16[32,2,2,1024]{3,2,1,0:T(2,128)(2,1)} %broadcast_in_dim.124), calls=%async_computation | async-start | bytes 524288 | tf_op jit(solution)/shard_map/all_to_all | solution.py:23
  31.4 12.7 %all-to-all-done = bf16[32,2,2,1024]{3,2,1,0:T(2,128)(2,1)S(1)} async-done(((bf16[32,2,2,1024]{3,2,1,0:T(2,128)(2,1)}), bf16[32,2,2,1024]{3,2,1,0:T(2,128)(2,1)S(1)}, u32[]{:S(2)}, u32[]{:S(2)}) %all-to-all-start) | async-done | bytes 262176 | tf_op jit(solution)/shard_map/all_to_all | solution.py:23
  44.4 40.4 %while.18 = (s32[]{:T(128)}, f32[64,2,1,8,128]{4,0,3,1,2:T(8,128)}, f32[64,2,1,8]{0,3,1,2:T(8,128)S(1)}, f32[64,2,1,8]{0,3,1,2:T(8,128)S(1)}, pred[2,4096]{1,0:T...) while((s32[]{:T(128)}, f32[64,2,1,8,128]{4,0,3,1,2:T(8,128)}, ...), condition=%wide.region_3.4_spmd.clone, body=%wide.region_0.3_spmd.clone.sunk | while | flops 275650560 | bytes 12402931 | solution.py:137
  44.4 1.5 bitcast_reduce_fusion.4
  46.9 1.7 %fusion.56 = f32[64,2,1,8,128]{4,0,3,1,2:T(8,128)S(1)} fusion(f32[2,512,64,8]{1,2,3,0:T(8,128)S(1)} %get-tuple-element.296, f32[64,2,8]{0,2,1:T(8,128)S(1)} %bitcast.175, pred[2,512]{1,0:T(4,128)(4,1)S(1)} %constant_dynamic-slice_fusion.2, f32[64,2,1,8,128]{4,0,3,1,2:T(8,128)S(1)} %copy-done.1, bf16[2,4096,128]{2,1,0:T(8,128)(2,1)} %get-tuple-element.331, ...), kind=kOutput, calls=%fused_computation.8.clone.1 | convolution fusion | flops 137232384 | bytes 3428357 | tf_op jit(solution)/shard_map/while/body/eval_jaxpr/nrkgb,rbkd->nrkgd/dot_general | solution.py:67
  49.5 1.5 bitcast_reduce_fusion.4
  52.0 1.7 %fusion.56 = f32[64,2,1,8,128]{4,0,3,1,2:T(8,128)S(1)} fusion(f32[2,512,64,8]{1,2,3,0:T(8,128)S(1)} %get-tuple-element.296, f32[64,2,8]{0,2,1:T(8,128)S(1)} %bitcast.175, pred[2,512]{1,0:T(4,128)(4,1)S(1)} %constant_dynamic-slice_fusion.2, f32[64,2,1,8,128]{4,0,3,1,2:T(8,128)S(1)} %copy-done.1, bf16[2,4096,128]{2,1,0:T(8,128)(2,1)} %get-tuple-element.331, ...), kind=kOutput, calls=%fused_computation.8.clone.1 | convolution fusion | flops 137232384 | bytes 3428357 | tf_op jit(solution)/shard_map/while/body/eval_jaxpr/nrkgb,rbkd->nrkgd/dot_general | solution.py:67
  54.5 1.5 bitcast_reduce_fusion.4
  57.0 1.7 %fusion.56 = f32[64,2,1,8,128]{4,0,3,1,2:T(8,128)S(1)} fusion(f32[2,512,64,8]{1,2,3,0:T(8,128)S(1)} %get-tuple-element.296, f32[64,2,8]{0,2,1:T(8,128)S(1)} %bitcast.175, pred[2,512]{1,0:T(4,128)(4,1)S(1)} %constant_dynamic-slice_fusion.2, f32[64,2,1,8,128]{4,0,3,1,2:T(8,128)S(1)} %copy-done.1, bf16[2,4096,128]{2,1,0:T(8,128)(2,1)} %get-tuple-element.331, ...), kind=kOutput, calls=%fused_computation.8.clone.1 | convolution fusion | flops 137232384 | bytes 3428357 | tf_op jit(solution)/shard_map/while/body/eval_jaxpr/nrkgb,rbkd->nrkgd/dot_general | solution.py:67
  59.5 1.5 bitcast_reduce_fusion.4
  62.1 1.7 %fusion.56 = f32[64,2,1,8,128]{4,0,3,1,2:T(8,128)S(1)} fusion(f32[2,512,64,8]{1,2,3,0:T(8,128)S(1)} %get-tuple-element.296, f32[64,2,8]{0,2,1:T(8,128)S(1)} %bitcast.175, pred[2,512]{1,0:T(4,128)(4,1)S(1)} %constant_dynamic-slice_fusion.2, f32[64,2,1,8,128]{4,0,3,1,2:T(8,128)S(1)} %copy-done.1, bf16[2,4096,128]{2,1,0:T(8,128)(2,1)} %get-tuple-element.331, ...), kind=kOutput, calls=%fused_computation.8.clone.1 | convolution fusion | flops 137232384 | bytes 3428357 | tf_op jit(solution)/shard_map/while/body/eval_jaxpr/nrkgb,rbkd->nrkgd/dot_general | solution.py:67
  64.6 1.5 bitcast_reduce_fusion.4
  67.1 1.7 %fusion.56 = f32[64,2,1,8,128]{4,0,3,1,2:T(8,128)S(1)} fusion(f32[2,512,64,8]{1,2,3,0:T(8,128)S(1)} %get-tuple-element.296, f32[64,2,8]{0,2,1:T(8,128)S(1)} %bitcast.175, pred[2,512]{1,0:T(4,128)(4,1)S(1)} %constant_dynamic-slice_fusion.2, f32[64,2,1,8,128]{4,0,3,1,2:T(8,128)S(1)} %copy-done.1, bf16[2,4096,128]{2,1,0:T(8,128)(2,1)} %get-tuple-element.331, ...), kind=kOutput, calls=%fused_computation.8.clone.1 | convolution fusion | flops 137232384 | bytes 3428357 | tf_op jit(solution)/shard_map/while/body/eval_jaxpr/nrkgb,rbkd->nrkgd/dot_general | solution.py:67
  69.6 1.5 bitcast_reduce_fusion.4
  72.2 1.7 %fusion.56 = f32[64,2,1,8,128]{4,0,3,1,2:T(8,128)S(1)} fusion(f32[2,512,64,8]{1,2,3,0:T(8,128)S(1)} %get-tuple-element.296, f32[64,2,8]{0,2,1:T(8,128)S(1)} %bitcast.175, pred[2,512]{1,0:T(4,128)(4,1)S(1)} %constant_dynamic-slice_fusion.2, f32[64,2,1,8,128]{4,0,3,1,2:T(8,128)S(1)} %copy-done.1, bf16[2,4096,128]{2,1,0:T(8,128)(2,1)} %get-tuple-element.331, ...), kind=kOutput, calls=%fused_computation.8.clone.1 | convolution fusion | flops 137232384 | bytes 3428357 | tf_op jit(solution)/shard_map/while/body/eval_jaxpr/nrkgb,rbkd->nrkgd/dot_general | solution.py:67
  74.7 1.5 bitcast_reduce_fusion.4
  77.2 1.7 %fusion.56 = f32[64,2,1,8,128]{4,0,3,1,2:T(8,128)S(1)} fusion(f32[2,512,64,8]{1,2,3,0:T(8,128)S(1)} %get-tuple-element.296, f32[64,2,8]{0,2,1:T(8,128)S(1)} %bitcast.175, pred[2,512]{1,0:T(4,128)(4,1)S(1)} %constant_dynamic-slice_fusion.2, f32[64,2,1,8,128]{4,0,3,1,2:T(8,128)S(1)} %copy-done.1, bf16[2,4096,128]{2,1,0:T(8,128)(2,1)} %get-tuple-element.331, ...), kind=kOutput, calls=%fused_computation.8.clone.1 | convolution fusion | flops 137232384 | bytes 3428357 | tf_op jit(solution)/shard_map/while/body/eval_jaxpr/nrkgb,rbkd->nrkgd/dot_general | solution.py:67
  79.7 1.5 bitcast_reduce_fusion.4
  82.3 1.7 %fusion.56 = f32[64,2,1,8,128]{4,0,3,1,2:T(8,128)S(1)} fusion(f32[2,512,64,8]{1,2,3,0:T(8,128)S(1)} %get-tuple-element.296, f32[64,2,8]{0,2,1:T(8,128)S(1)} %bitcast.175, pred[2,512]{1,0:T(4,128)(4,1)S(1)} %constant_dynamic-slice_fusion.2, f32[64,2,1,8,128]{4,0,3,1,2:T(8,128)S(1)} %copy-done.1, bf16[2,4096,128]{2,1,0:T(8,128)(2,1)} %get-tuple-element.331, ...), kind=kOutput, calls=%fused_computation.8.clone.1 | convolution fusion | flops 137232384 | bytes 3428357 | tf_op jit(solution)/shard_map/while/body/eval_jaxpr/nrkgb,rbkd->nrkgd/dot_general | solution.py:67
  85.3 0.8 reshape.179
  86.2 4.2 %all-to-all-start.2 = ((f32[32,1,1024]{2,1,0:T(1,128)}), f32[32,1,1024]{2,1,0:T(1,128)S(1)}, u32[]{:S(2)}, u32[]{:S(2)}) async-start(f32[32,1,1024]{2,1,0:T(1,128)} %reshape.179), calls=%async_computation.2 | async-start | bytes 262144 | tf_op jit(solution)/shard_map/all_to_all | solution.py:23
  90.4 10.7 %all-to-all-done.2 = f32[32,1,1024]{2,1,0:T(1,128)S(1)} async-done(((f32[32,1,1024]{2,1,0:T(1,128)}), f32[32,1,1024]{2,1,0:T(1,128)S(1)}, u32[]{:S(2)}, u32[]{:S(2)}) %all-to-all-start.2) | async-done | bytes 131104 | tf_op jit(solution)/shard_map/all_to_all | solution.py:23
  101.6 1.0 reduce.15
  102.9 14.0 %all_to_all.35 = f32[32,1,1024]{2,1,0:T(1,128)S(1)} all-to-all(f32[32,1,1024]{2,1,0:T(1,128)S(1)} %reshape.181), channel_id=1, replica_groups=mesh['ctx'=32,'tp'=8] {'ctx'}, dimensions={0} | all-to-all | bytes 262144 | tf_op jit(solution)/shard_map/all_to_all | solution.py:23
  117.0 1.0 reduce.16
  118.8 20.2 %all_to_all.36 = f32[32,2,2,1,8,128]{5,1,4,2,3,0:T(2,128)S(1)} all-to-all(f32[32,2,2,1,8,128]{5,1,4,2,3,0:T(2,128)S(1)} %copy.38), channel_id=1, replica_groups=mesh['ctx'=32,'tp'=8] {'ctx'}, dimensions={0} | all-to-all | bytes 1048576 | tf_op jit(solution)/shard_map/all_to_all | solution.py:56
  139.2 18.5 %all_to_all.37 = bf16[32,2,2,1,8,128]{5,4,1,2,3,0:T(8,128)(2,1)S(1)} all-to-all(bf16[32,2,2,1,8,128]{5,4,1,2,3,0:T(8,128)(2,1)S(1)} %broadcast_in_dim.131), channel_id=1, replica_groups=mesh['ctx'=32,'tp'=8] {'ctx'}, dimensions={0} | all-to-all | bytes 524288 | tf_op jit(solution)/shard_map/all_to_all | solution.py:23
  158.2 9.4 %all_to_all.38 = f32[8,8,2,256]{3,1,2,0:T(8,128)S(1)} all-to-all(f32[8,8,2,256]{3,1,2,0:T(8,128)S(1)} %fusion.29), channel_id=1, replica_groups=mesh['ctx'=32,'tp'=8] {'tp'}, dimensions={0} | all-to-all | bytes 262144 | tf_op jit(solution)/shard_map/all_to_all | solution.py:56
  (119 shorter events, 21.5 us)
Async XLA Ops:
  0.6 157.3 %copy-start = (bf16[1024,256]{1,0:T(8,128)(2,1)S(1)}, bf16[1024,256]{1,0:T(8,128)(2,1)}, u32[]{:S(2)}) copy-start(bf16[1024,256]{1,0:T(8,128)(2,1)} %param.17) | copy-start | bytes 1572868
  3.1 22.5 %all-to-all-start.1 = ((bf16[32,4,2,128]{3,2,1,0:T(2,128)(2,1)}), bf16[32,4,2,128]{3,2,1,0:T(2,128)(2,1)S(1)}, u32[]{:S(2)}, u32[]{:S(2)}) async-start(bf16[32,4,2,128]{3,2,1,0:T(2,128)(2,1)} %pad_maximum_fusion), calls=%async_computation.1 | async-start | bytes 131072 | tf_op jit(solution)/shard_map/all_to_all | solution.py:17
  27.2 16.9 %all-to-all-start = ((bf16[32,2,2,1024]{3,2,1,0:T(2,128)(2,1)}), bf16[32,2,2,1024]{3,2,1,0:T(2,128)(2,1)S(1)}, u32[]{:S(2)}, u32[]{:S(2)}) async-start(bf16[32,2,2,1024]{3,2,1,0:T(2,128)(2,1)} %broadcast_in_dim.124), calls=%async_computation | async-start | bytes 524288 | tf_op jit(solution)/shard_map/all_to_all | solution.py:23
  31.3 53.6 %copy-start.5 = (bf16[2,2,128]{2,1,0:T(2,128)(2,1)}, bf16[2,2,128]{2,1,0:T(2,128)(2,1)S(1)}, u32[]{:S(2)}) copy-start(bf16[2,2,128]{2,1,0:T(2,128)(2,1)S(1)} %get-tuple-element.216) | copy-start | bytes 3076
  31.4 86.7 %copy-start.4 = (bf16[2,2,128]{2,1,0:T(2,128)(2,1)}, bf16[2,2,128]{2,1,0:T(2,128)(2,1)S(1)}, u32[]{:S(2)}) copy-start(bf16[2,2,128]{2,1,0:T(2,128)(2,1)S(1)} %get-tuple-element.215) | copy-start | bytes 3076
  45.9 1.0 copy-start.1
  48.7 0.8 copy-start.2
  50.9 1.0 copy-start.1
  53.7 0.8 copy-start.2
  56.0 1.0 copy-start.1
  58.8 0.8 copy-start.2
  61.0 1.0 copy-start.1
  63.8 0.8 copy-start.2
  66.1 1.0 copy-start.1
  68.8 0.8 copy-start.2
  71.1 1.0 copy-start.1
  73.9 0.8 copy-start.2
  76.2 1.0 copy-start.1
  78.9 0.8 copy-start.2
  81.2 1.0 copy-start.1
  84.0 0.8 copy-start.2
  85.0 33.1 %copy-start.3 = (f32[64,2,1,8,128]{4,0,3,1,2:T(8,128)S(1)}, f32[64,2,1,8,128]{4,0,3,1,2:T(8,128)}, u32[]{:S(2)}) copy-start(f32[64,2,1,8,128]{4,0,3,1,2:T(8,128)} %get-tuple-element.144) | copy-start | bytes 1572868
  86.2 14.9 %all-to-all-start.2 = ((f32[32,1,1024]{2,1,0:T(1,128)}), f32[32,1,1024]{2,1,0:T(1,128)S(1)}, u32[]{:S(2)}, u32[]{:S(2)}) async-start(f32[32,1,1024]{2,1,0:T(1,128)} %reshape.179), calls=%async_computation.2 | async-start | bytes 262144 | tf_op jit(solution)/shard_map/all_to_all | solution.py:23
where the time goes:
time: 170 us; the launch traced here: 168 us
  blocking collectives  62.1 us (37%)
  waiting for transfers between devices  31.6 us (19%)
  matrix products  26.5 us (16%)
  starting transfers between devices  20.8 us (12%)
  local copies, waits for them, and re-layouts  14.8 us (9%)
  other arithmetic  10.9 us (6%)
    all_to_all x2, blocking collectives, copy_for_each(): lax.all_to_all(jnp.broadcast_to(array[None], (size, *array.shape)), axis,...  32.6 us
    all_to_all x2, blocking collectives, sum_at_owner(): parts = lax.all_to_all(cut_along(array, dim, size), axis, 0, 0, tiled=True)  29.5 us
    all_to_all x2, waiting for transfers between devices, copy_for_each(): lax.all_to_all(jnp.broadcast_to(array[None], (size, *array.shape)), axis,...  23.4 us
    dot_general x9, matrix products, online_step(): jnp.einsum('nrkgb,rbkd->nrkgd', weights.astype(jnp.bfloat16), value_block...  14.3 us
    all_to_all x1, starting transfers between devices, in_one_piece(): lax.all_to_all(both, axis, split_axis=split_dim, concat_axis=concat_dim,...  12.7 us
    dot_general x8, matrix products, visit(): jnp.einsum('nrkgd,rbkd->nrkgb', grouped, key_slab, preferred_element_type...  11.7 us
    while x40, local copies, waits for them, and re-layouts  9.04 us
    all_to_all x1, waiting for transfers between devices, in_one_piece(): lax.all_to_all(both, axis, split_axis=split_dim, concat_axis=concat_dim,...  8.19 us
  transfers between devices with their start and end apart: 3, of which 3 were waited for; matrix products, arithmetic and copies ran while one was open for 1% of the time, Pallas kernels for 0%

commit v1 on v0

v1 whole, which is shorter than its diff:
```python
import functools
import math

import jax
import jax.numpy as jnp
from jax import lax
from jax.experimental import pallas as pl
from jax.experimental.pallas import tpu as pltpu
from jax.sharding import PartitionSpec as P

HD = 128
FLOOR = -1e30
KEY_BLOCK = 512
MESH = pl.DeviceIdType.MESH


def kernel(
    members,
    groups,
    q_ref,
    nk_ref,
    nv_ref,
    ck_ref,
    cv_ref,
    hist_ref,
    owner_ref,
    w_ref,
    out_ref,
    sk_ref,
    sv_ref,
    kbuf,
    vbuf,
    wbuf,
    qtmp,
    ktail,
    qall,
    kvall,
    scores,
    acc,
    ready,
    lse,
    osend,
    lsend,
    orecv,
    lrecv,
    abuf,
    psend,
    precv,
    load_sem,
    qs_sem,
    qr_sem,
    ks_sem,
    kr_sem,
    os_sem,
    or_sem,
    ls_sem,
    lr_sem,
    as_sem,
    ar_sem,
    ps_sem,
    pr_sem,
):
    me = lax.axis_index("ctx")
    mine = lax.axis_index("tp")
    requests, history = ck_ref.shape[:2]
    page = q_ref.shape[0]
    heads = q_ref.shape[2] // HD
    turn = page * members
    rows = turn * heads
    half_size = history // 2
    tail = kbuf.shape[1] - history
    factor = math.log2(math.e) / math.sqrt(HD)

    def load(r):
        return (
            pltpu.make_async_copy(ck_ref.at[r], kbuf.at[r, pl.ds(0, history)], load_sem.at[2 * r]),
            pltpu.make_async_copy(cv_ref.at[r], vbuf.at[r, pl.ds(0, history)], load_sem.at[2 * r + 1]),
        )

    load_w = pltpu.make_async_copy(w_ref, wbuf, load_sem.at[2 * requests])
    for r in range(requests):
        for copy in load(r):
            copy.start()
    load_w.start()

    barrier = pltpu.get_barrier_semaphore()

    def greet(axis, size, position):
        def one(k, c):
            pl.semaphore_signal(
                barrier, inc=1, device_id={axis: lax.rem(position + k, size)}, device_id_type=MESH
            )
            return c

        lax.fori_loop(1, size, one, 0)

    greet("ctx", members, me)
    greet("tp", groups, mine)

    for t in range(page):
        row = q_ref[t].astype(jnp.float32)
        for h in range(heads):
            for r in range(requests):
                qtmp[r, pl.ds(t * heads + h, 1), :] = row[r : r + 1, h * HD : (h + 1) * HD]
    qall[me] = qtmp[...].astype(qall.dtype)
    kvall[me, 0] = nk_ref[...]
    kvall[me, 1] = nv_ref[...]
    pl.semaphore_wait(barrier, members - 1 + groups - 1)

    def to(k):
        return lax.rem(me + k, members)

    def query_copy(r, source, target):
        return pltpu.make_async_remote_copy(
            src_ref=qall.at[source, r],
            dst_ref=qall.at[source, r],
            send_sem=qs_sem.at[r, target],
            recv_sem=qr_sem.at[r, source],
            device_id={"ctx": target},
            device_id_type=MESH,
        )

    def page_copy(source, target):
        return pltpu.make_async_remote_copy(
            src_ref=kvall.at[source],
            dst_ref=kvall.at[source],
            send_sem=ks_sem.at[target],
            recv_sem=kr_sem.at[source],
            device_id={"ctx": target},
            device_id_type=MESH,
        )

    def for_peers(fn):
        def one(k, c):
            fn(to(k))
            return c

        lax.fori_loop(1, members, one, 0)

    for r in range(requests):
        for_peers(lambda peer: query_copy(r, me, peer).start())
    for_peers(lambda peer: page_copy(me, peer).start())

    for r in range(requests):
        for source, target in ((nk_ref, kbuf), (nv_ref, vbuf)):
            ktail[...] = jnp.zeros_like(ktail)
            ktail[pl.ds(0, page), :] = source[r].astype(jnp.float32)
            target[r, pl.ds(history, tail), :] = ktail[...].astype(target.dtype)

    ones = jnp.ones((KEY_BLOCK, HD), jnp.bfloat16)
    row_token = lax.broadcasted_iota(jnp.int32, (rows, tail), 0) // heads
    tail_lane = lax.broadcasted_iota(jnp.int32, (rows, tail), 1)
    tail_visible = (tail_lane < page) & (tail_lane + page * me <= row_token)
    token_row = lax.broadcasted_iota(jnp.int32, (turn // 2, HD), 0)
    token_lane = lax.broadcasted_iota(jnp.int32, (turn // 2, HD), 1)

    def piece_copy(source, target):
        return (
            pltpu.make_async_remote_copy(
                src_ref=osend.at[target],
                dst_ref=orecv.at[source],
                send_sem=os_sem.at[target],
                recv_sem=or_sem.at[source],
                device_id={"ctx": target},
                device_id_type=MESH,
            ),
            pltpu.make_async_remote_copy(
                src_ref=lsend.at[target],
                dst_ref=lrecv.at[source],
                send_sem=ls_sem.at[target],
                recv_sem=lr_sem.at[source],
                device_id={"ctx": target},
                device_id_type=MESH,
            ),
        )

    dot_nt = functools.partial(
        lax.dot_general,
        dimension_numbers=(((1,), (1,)), ((), ())),
        preferred_element_type=jnp.float32,
    )
    for r in range(requests):
        for copy in load(r):
            copy.wait()
        for_peers(lambda peer: query_copy(r, peer, me).wait_recv())
        queries = qall[:, r].reshape(rows, HD)

        def score(b, peak):
            offset = pl.multiple_of(b * KEY_BLOCK, KEY_BLOCK)
            block = dot_nt(queries, kbuf[r, pl.ds(offset, KEY_BLOCK), :])
            first = jnp.where(
                offset < half_size,
                me * half_size + offset,
                (2 * members - 1 - me) * half_size + offset - half_size,
            )
            lane = lax.broadcasted_iota(jnp.int32, (1, KEY_BLOCK), 1)
            block = block + jnp.where(lane < hist_ref[r] - first, 0.0, FLOOR)
            scores[:, pl.ds(offset, KEY_BLOCK)] = block
            for p in range(KEY_BLOCK // HD):
                peak = jnp.maximum(peak, block[:, p * HD : (p + 1) * HD])
            return peak

        last = dot_nt(queries, kbuf[r, pl.ds(history, tail), :])
        last = jnp.where(tail_visible, last, FLOOR)
        acc_peak = lax.fori_loop(0, history // KEY_BLOCK, score, last)
        peak = jnp.max(acc_peak, axis=1, keepdims=True)

        weights = jnp.exp2((last - peak) * factor).astype(jnp.bfloat16)
        values = jnp.concatenate([vbuf[r, pl.ds(history, tail), :], ones[:tail]], axis=1)
        acc[...] = jnp.dot(weights, values, preferred_element_type=jnp.float32)

        def add(b, c):
            offset = pl.multiple_of(b * KEY_BLOCK, KEY_BLOCK)
            weights = jnp.exp2((scores[:, pl.ds(offset, KEY_BLOCK)] - peak) * factor).astype(jnp.bfloat16)
            values = jnp.concatenate([vbuf[r, pl.ds(offset, KEY_BLOCK), :], ones], axis=1)
            acc[...] += jnp.dot(weights, values, preferred_element_type=jnp.float32)
            return c

        lax.fori_loop(0, history // KEY_BLOCK, add, 0)
        total = acc[:, HD:]
        lse[...] = peak * factor + jnp.log2(total)
        ready[...] = acc[:, :HD] / total

        for h in range(heads):
            for half in range(2):
                target = h * 4 + half * 2 + r
                picked = pl.ds(half * (turn // 2) * heads + h, turn // 2, stride=heads)
                osend[target] = ready[picked, :].astype(osend.dtype)
                lsend[target] = jnp.sum(
                    jnp.where(token_row == token_lane, lse[picked, :], 0.0), axis=0, keepdims=True
                )

        def send(k, c):
            target = lax.rem((me // requests) + k, members // requests) * requests + r

            @pl.when(target != me)
            def _():
                for copy in piece_copy(me, target):
                    copy.start()

            return c

        lax.fori_loop(0, members // requests, send, 0)

    orecv[me] = osend[me]
    lrecv[me] = lsend[me]

    def arrived(peer):
        for copy in piece_copy(peer, me):
            copy.wait_recv()

    for_peers(arrived)
    levels = lrecv[...].reshape(members, HD)
    levels = jnp.concatenate([levels, jnp.full((HD - members, HD), FLOOR, jnp.float32)], axis=0)
    levels = levels.T[: turn // 2]
    share = jnp.exp2(levels - jnp.max(levels, axis=1, keepdims=True))
    share = share / jnp.sum(share, axis=1, keepdims=True)
    done = jnp.zeros((turn // 2, HD), jnp.float32)
    for s in range(members):
        done = done + share[:, s : s + 1] * orecv[s].astype(jnp.float32)
    head = me // 4
    first_row = pl.multiple_of((lax.rem(me, 2) * 2 + lax.rem(me // 2, 2)) * (turn // 2), turn // 2)
    abuf[head, pl.ds(first_row, turn // 2), :] = done.astype(abuf.dtype)

    def finished_copy(source, target):
        start = pl.multiple_of((lax.rem(source, 2) * 2 + lax.rem(source // 2, 2)) * (turn // 2), turn // 2)
        place = abuf.at[source // 4, pl.ds(start, turn // 2)]
        return pltpu.make_async_remote_copy(
            src_ref=place,
            dst_ref=place,
            send_sem=as_sem.at[target],
            recv_sem=ar_sem.at[source],
            device_id={"ctx": target},
            device_id_type=MESH,
        )

    for_peers(lambda peer: finished_copy(me, peer).start())
    load_w.wait()
    for_peers(lambda peer: page_copy(peer, me).wait_recv())
    for r in range(requests):
        source = jnp.int32(0)
        for b in range(members):
            source = jnp.maximum(source, jnp.where(owner_ref[r, b] == me, b, 0))
        sk_ref[r] = kvall[source, 0, r]
        sv_ref[r] = kvall[source, 1, r]
    for_peers(lambda peer: finished_copy(peer, me).wait_recv())

    rows_in = jnp.concatenate([abuf[h] for h in range(heads)], axis=1)
    part = jnp.dot(rows_in, wbuf[...], preferred_element_type=jnp.float32)
    share_rows = turn // groups
    for g in range(groups):
        psend[g] = jnp.concatenate(
            [part[r * turn + g * share_rows : r * turn + (g + 1) * share_rows] for r in range(requests)], axis=0
        ).astype(psend.dtype)

    def part_copy(source, target):
        return pltpu.make_async_remote_copy(
            src_ref=psend.at[target],
            dst_ref=precv.at[source],
            send_sem=ps_sem.at[target],
            recv_sem=pr_sem.at[source],
            device_id={"tp": target},
            device_id_type=MESH,
        )

    def for_groups(fn):
        def one(k, c):
            fn(lax.rem(mine + k, groups))
            return c

        lax.fori_loop(1, groups, one, 0)

    for_groups(lambda peer: part_copy(mine, peer).start())
    precv[mine] = psend[mine]
    for_groups(lambda peer: part_copy(peer, mine).wait_recv())
    full = precv[0].astype(jnp.float32)
    for g in range(1, groups):
        full = full + precv[g].astype(jnp.float32)
    out_ref[...] = full

    def drained(peer):
        for r in range(requests):
            query_copy(r, me, peer).wait_send()
        page_copy(me, peer).wait_send()
        for copy in piece_copy(me, peer):
            copy.wait_send()
        finished_copy(me, peer).wait_send()

    for_peers(drained)
    for_groups(lambda peer: part_copy(mine, peer).wait_send())


def on_device(queries, new_keys, new_values, cache_keys, cache_values, hist_len, page_owner, out_weight):
    members = lax.axis_size("ctx")
    groups = lax.axis_size("tp")
    page, requests, width = queries.shape
    history = cache_keys.shape[1]
    heads = width // HD
    turn = page * members
    columns = out_weight.shape[1]
    vmem = pl.BlockSpec(memory_space=pltpu.VMEM)
    smem = pl.BlockSpec(memory_space=pltpu.SMEM)
    anywhere = pl.BlockSpec(memory_space=pl.ANY)
    bf16, f32 = jnp.bfloat16, jnp.float32
    dma = pltpu.SemaphoreType.DMA
    full, kept_keys, kept_values = pl.pallas_call(
        functools.partial(kernel, members, groups),
        out_shape=(
            jax.ShapeDtypeStruct((requests * (turn // groups), columns), f32),
            jax.ShapeDtypeStruct(new_keys.shape, bf16),
            jax.ShapeDtypeStruct(new_keys.shape, bf16),
        ),
        in_specs=[vmem, vmem, vmem, anywhere, anywhere, smem, smem, anywhere],
        out_specs=[vmem, vmem, vmem],
        scratch_shapes=[
            pltpu.VMEM((requests, history + HD, HD), bf16),
            pltpu.VMEM((requests, history + HD, HD), bf16),
            pltpu.VMEM(out_weight.shape, bf16),
            pltpu.VMEM((requests, page * heads, HD), f32),
            pltpu.VMEM((HD, HD), f32),
            pltpu.VMEM((members, requests, page * heads, HD), bf16),
            pltpu.VMEM((members, 2, *new_keys.shape), bf16),
            pltpu.VMEM((turn * heads, history), f32),
            pltpu.VMEM((turn * heads, 2 * HD), f32),
            pltpu.VMEM((turn * heads, HD), f32),
            pltpu.VMEM((turn * heads, HD), f32),
            pltpu.VMEM((members, turn // 2, HD), bf16),
            pltpu.VMEM((members, 1, HD), f32),
            pltpu.VMEM((members, turn // 2, HD), bf16),
            pltpu.VMEM((members, 1, HD), f32),
            pltpu.VMEM((heads, requests * turn, HD), bf16),
            pltpu.VMEM((groups, requests * (turn // groups), columns), bf16),
            pltpu.VMEM((groups, requests * (turn // groups), columns), bf16),
            dma((2 * requests + 1,)),
            dma((requests, members)),
            dma((requests, members)),
            dma((members,)),
            dma((members,)),
            dma((members,)),
            dma((members,)),
            dma((members,)),
            dma((members,)),
            dma((members,)),
            dma((members,)),
            dma((groups,)),
            dma((groups,)),
        ],
        compiler_params=pltpu.CompilerParams(collective_id=0, has_side_effects=True),
    )(queries, new_keys, new_values, cache_keys, cache_values, hist_len, page_owner, out_weight)
    attended = full.astype(bf16).reshape(requests, turn // groups, columns).transpose(1, 0, 2)
    return (attended, kept_keys[None], kept_values[None])


def solution(mesh):
    return jax.shard_map(
        on_device,
        mesh=mesh,
        in_specs=(
            P("ctx", None, "tp"),
            P(None, "ctx", "tp"),
            P(None, "ctx", "tp"),
            P(None, "ctx", "tp"),
            P(None, "ctx", "tp"),
            P(),
            P(),
            P("tp", "ctx"),
        ),
        out_specs=(P("tp", None, "ctx"), P("ctx", None, None, "tp"), P("ctx", None, None, "tp")),
        check_vma=False,
    )
```

time: 170 us -> 59.4 us (0.35)
  blocking collectives: 62.1 us -> 0 us
  Pallas kernels: 0 us -> 54.6 us
  waiting for transfers between devices: 31.6 us -> 0 us
  matrix products: 26.5 us -> 0 us
  starting transfers between devices: 20.8 us -> 0 us
  local copies, waits for them, and re-layouts: 14.8 us -> 3.05 us
  other arithmetic: 10.9 us -> 0.72 us
    all_to_all x4 -> x0, blocking collectives: 62.1 us -> none  [the longest x2 32.6 us: copy_for_each(): lax.all_to_all(jnp.broadcast_to(array[None], (size, *array.shape)), axis,...]
    pallas_call x0 -> x1, Pallas kernels: none -> 54.6 us  [on_device(): pl.pallas_call(functools.partial(kernel, members, groups), out_shape=(jax...]
    all_to_all x3 -> x0, waiting for transfers between devices: 31.6 us -> none  [the longest x2 23.4 us: copy_for_each(): lax.all_to_all(jnp.broadcast_to(array[None], (size, *array.shape)), axis,...]
    dot_general x19 -> x0, matrix products: 26.5 us -> none  [the longest x9 14.3 us: online_step(): jnp.einsum('nrkgb,rbkd->nrkgd', weights.astype(jnp.bfloat16), value_block...]
    all_to_all x3 -> x0, starting transfers between devices: 20.8 us -> none  [the longest x1 12.7 us: in_one_piece(): lax.all_to_all(both, axis, split_axis=split_dim, concat_axis=concat_dim,...]
    while x40 -> x0, local copies, waits for them, and re-layouts: 9.04 us -> none
    reduce_sum x14 -> x0, other arithmetic: 6.33 us -> none  [the longest x9 5.24 us: online_step(): running_total = running_total * shrink + jnp.sum(weights, axis=-1)]
    all_to_all x2 -> x0, other arithmetic: 1.9 us -> none  [copy_for_each(): lax.all_to_all(jnp.broadcast_to(array[None], (size, *array.shape)), axis,...]
  transfers between devices with their start and end apart: 3 -> 0, of which waited for: 3 -> 0; matrix products, arithmetic and copies ran while one was open for 1% -> 0% of each run, Pallas kernels for 0% -> 0%
where the time goes in v1:
time: 59.4 us; the launch traced here: 59 us
  Pallas kernels  54.6 us (92%)
  local copies, waits for them, and re-layouts  3.05 us (5%)
  other arithmetic  0.72 us (1%)
  between operations  0.64 us (1%)
    pallas_call x1, Pallas kernels, on_device(): pl.pallas_call(functools.partial(kernel, members, groups), out_shape=(jax...  54.6 us
    unnamed x2, local copies, waits for them, and re-layouts  2.45 us

profile of v1, /device:TPU:1, one launch (start us, length us, event | category | flops | bytes accessed | tf_op | source)
XLA Modules:
  0.0 59.0 jit_solution(3238682820249167792)
XLA Ops:
  0.6 54.6 %shard_map.103 = (f32[16,256]{1,0:T(8,128)}, bf16[2,2,128]{2,1,0:T(2,128)(2,1)}, bf16[2,2,128]{2,1,0:T(2,128)(2,1)}) custom-call(bf16[2,2,1024]{2,1,0:T(2,128)(2,1)} %q_ref.1, bf16[2,2,128]{2,1,0:T(2,128)(2,1)} %nk_ref.1, bf16[2,2,128]{2,1,0:T(2,128)(2,1)} %nv_ref.1, bf16[2,4096,128]{2,1,0:T(8,128)(2,1)} %ck_ref.1, bf16[2,4096,128]{2,1,0:T(8,128)(2,1)} %cv_ref.1, ...), custom_call_target="tpu_custom_call" | custom-call | tf_op jit(solution)/shard_map/pallas_call | solution.py:346
  55.2 0.7 %convert_bitcast_fusion = bf16[2,8,256]{2,1,0:T(8,128)(2,1)S(1)} fusion(f32[16,256]{1,0:T(8,128)} %get-tuple-element.6), kind=kLoop, calls=%fused_computation.1 | loop fusion | flops 4096 | bytes 24576 | tf_op jit(solution)/shard_map/reshape | solution.py:390
  56.0 0.6 %copy.13 = bf16[2,8,256]{2,0,1:T(2,128)(2,1)} copy(bf16[2,8,256]{2,1,0:T(8,128)(2,1)S(1)} %convert_bitcast_fusion) | data formatting | bytes 16384 | tf_op jit(solution)/shard_map/reshape | solution.py:390
  56.6 1.2 %copy.16 = bf16[1,2,2,128]{3,2,1,0:T(2,128)(2,1)} copy(bf16[1,2,2,128]{3,2,1,0:T(2,128)(2,1)} %bitcast.9) | data formatting | bytes 2048
  57.8 1.2 %copy.17 = bf16[1,2,2,128]{3,2,1,0:T(2,128)(2,1)} copy(bf16[1,2,2,128]{3,2,1,0:T(2,128)(2,1)} %bitcast.8) | data formatting | bytes 2048

commit v2 on v1

v2 whole, which is shorter than its diff:
```python
import functools
import math

import jax
import jax.numpy as jnp
from jax import lax
from jax.experimental import pallas as pl
from jax.experimental.pallas import tpu as pltpu
from jax.sharding import PartitionSpec as P

HD = 128
FLOOR = -1e30
MESH = pl.DeviceIdType.MESH


def kernel(
    members,
    groups,
    q_ref,
    nk_ref,
    nv_ref,
    ck_ref,
    cv_ref,
    hist_ref,
    owner_ref,
    w_ref,
    out_ref,
    sk_ref,
    sv_ref,
    kbuf,
    vbuf,
    wbuf,
    qtmp,
    ktail,
    qown,
    qall,
    kvall,
    scores,
    acc,
    ready,
    lse,
    osend,
    lsend,
    orecv,
    lrecv,
    abuf,
    psend,
    precv,
    load_sem,
    chip_send,
    chip_recv,
    q_send,
    q_recv,
    page_send,
    page_recv,
    o_send,
    o_recv,
    l_send,
    l_recv,
    f_send,
    f_recv,
    p_send,
    p_recv,
):
    me = lax.axis_index("ctx")
    mine = lax.axis_index("tp")
    requests, history = ck_ref.shape[:2]
    page = q_ref.shape[0]
    heads = q_ref.shape[2] // HD
    turn = page * members
    chunk = turn // 2
    rows = chunk * heads
    half_size = history // 2
    owners = members // requests
    near = members // 2
    share_rows = turn // groups
    tail = kbuf.shape[0] - 2 * history
    factor = math.log2(math.e) / math.sqrt(HD)

    r = lax.rem(me, 2)
    other = 1 - r
    partner = me + 1 - 2 * r
    own = me // 2
    side = own // heads

    load_k = pltpu.make_async_copy(ck_ref.at[r], kbuf.at[pl.ds(0, history)], load_sem.at[0])
    load_v = pltpu.make_async_copy(cv_ref.at[r], vbuf.at[pl.ds(0, history)], load_sem.at[1])
    load_w = pltpu.make_async_copy(w_ref, wbuf.at[r], load_sem.at[2])
    load_k.start()
    load_v.start()
    load_w.start()

    barrier = pltpu.get_barrier_semaphore()

    def greet(**device):
        pl.semaphore_signal(barrier, inc=1, device_id=device, device_id_type=MESH)

    def greet_ctx(k, c):
        greet(ctx=lax.rem(me + k, members))
        return c

    def greet_tp(k, c):
        for j in range(requests):
            greet(ctx=me - r + j, tp=lax.rem(mine + k, groups))
        return c

    lax.fori_loop(1, members, greet_ctx, 0)
    lax.fori_loop(1, groups, greet_tp, 0)

    for t in range(page):
        row = q_ref[t].astype(jnp.float32)
        for h in range(heads):
            for s in range(requests):
                qtmp[s, pl.ds(t * heads + h, 1), :] = row[s : s + 1, h * HD : (h + 1) * HD]
    qown[...] = qtmp[...].astype(qown.dtype)
    qall[me] = qown[r]
    kvall[me, 0] = nk_ref[...]
    kvall[me, 1] = nv_ref[...]
    pl.semaphore_wait(barrier, members - 1 + requests * (groups - 1))

    def remote(src, dst, send_sem, recv_sem, **device):
        return pltpu.make_async_remote_copy(
            src_ref=src, dst_ref=dst, send_sem=send_sem, recv_sem=recv_sem, device_id=device, device_id_type=MESH
        )

    def landed(ref, sem):
        pltpu.make_async_copy(ref, ref, sem).wait()

    def send_query(peer, where):
        remote(qown.at[lax.rem(peer, 2)], qall.at[me], q_send, q_recv.at[where], ctx=peer).start()

    def near_query(k, c):
        send_query(side * near + lax.rem(lax.rem(me, near) + k, near), 0)
        return c

    def far_query(k, c):
        send_query((1 - side) * near + lax.rem(lax.rem(me, near) + k, near), 1)
        return c

    lax.fori_loop(1, near, near_query, 0)
    lax.fori_loop(0, near, far_query, 0)

    history_slab = pl.ds(history, history)
    give_k = remote(ck_ref.at[other], kbuf.at[history_slab], chip_send.at[0], chip_recv.at[0], ctx=partner)
    give_v = remote(cv_ref.at[other], vbuf.at[history_slab], chip_send.at[1], chip_recv.at[1], ctx=partner)
    give_w = remote(w_ref, wbuf.at[r], chip_send.at[2], chip_recv.at[2], ctx=partner)
    give_page = remote(kvall.at[me], kvall.at[me], chip_send.at[3], chip_recv.at[3], ctx=partner)
    give_page.start()
    give_k.start()
    give_v.start()
    give_w.start()

    give_page.wait_recv()
    for source, target in ((0, kbuf), (1, vbuf)):
        ktail[...] = jnp.zeros_like(ktail)
        for j in range(2):
            ktail[pl.ds(j * page, page), :] = kvall[me - r + j, source, r].astype(jnp.float32)
        target[pl.ds(2 * history, tail), :] = ktail[...].astype(target.dtype)

    ones = jnp.ones((history, HD), jnp.bfloat16)
    row_token = lax.broadcasted_iota(jnp.int32, (rows, tail), 0) // heads
    tail_lane = lax.broadcasted_iota(jnp.int32, (rows, tail), 1)
    token_row = lax.broadcasted_iota(jnp.int32, (chunk, HD), 0)
    token_lane = lax.broadcasted_iota(jnp.int32, (chunk, HD), 1)
    slot = lax.broadcasted_iota(jnp.int32, (1, history), 1)

    def bias_of(device):
        low = hist_ref[r] - device * half_size
        high = hist_ref[r] - (2 * members - 1 - device) * half_size + half_size
        return jnp.where(slot < jnp.where(slot < half_size, low, high), 0.0, FLOOR)

    dot_nt = functools.partial(
        lax.dot_general,
        dimension_numbers=(((1,), (1,)), ((), ())),
        preferred_element_type=jnp.float32,
    )

    def score(queries, b, device, peak):
        block = dot_nt(queries, kbuf[b * history : (b + 1) * history, :]) + bias_of(device)
        scores[:, b * history : (b + 1) * history] = block
        for p in range(history // HD):
            peak = jnp.maximum(peak, block[:, p * HD : (p + 1) * HD])
        return peak

    def weigh(b, peak):
        weights = jnp.exp2((scores[:, b * history : (b + 1) * history] - peak) * factor).astype(jnp.bfloat16)
        values = jnp.concatenate([vbuf[b * history : (b + 1) * history, :], ones], axis=1)
        return jnp.dot(weights, values, preferred_element_type=jnp.float32)

    for turn_half in range(2):
        which = side if turn_half == 0 else 1 - side
        first = which * near
        if turn_half == 0:
            landed(qall.at[pl.ds(0, near - 1)], q_recv.at[0])
            load_k.wait()
        else:
            landed(qall.at[pl.ds(0, near)], q_recv.at[1])
        queries = qall[pl.ds(first, near)].reshape(rows, HD)
        last = dot_nt(queries, kbuf[2 * history :, :])
        visible = (tail_lane < 2 * page) & (tail_lane + 2 * page * own <= row_token + which * chunk)
        last = jnp.where(visible, last, FLOOR)
        peak = score(queries, 0, me, last)
        if turn_half == 0:
            give_k.wait_recv()
        peak = score(queries, 1, partner, peak)
        peak = jnp.max(peak, axis=1, keepdims=True)
        weights = jnp.exp2((last - peak) * factor).astype(jnp.bfloat16)
        values = jnp.concatenate([vbuf[2 * history :, :], ones[:tail]], axis=1)
        acc[...] = jnp.dot(weights, values, preferred_element_type=jnp.float32)
        if turn_half == 0:
            load_v.wait()
        acc[...] += weigh(0, peak)
        if turn_half == 0:
            give_v.wait_recv()
        acc[...] += weigh(1, peak)
        total = acc[:, HD:]
        lse[...] = peak * factor + jnp.log2(total)
        ready[...] = acc[:, :HD] / total

        base = (1 - which) * heads
        for h in range(heads):
            picked = pl.ds(h, chunk, stride=heads)
            osend[base + h] = ready[picked, :].astype(osend.dtype)
            lsend[base + h] = jnp.sum(jnp.where(token_row == token_lane, lse[picked, :], 0.0), axis=0, keepdims=True)

        def send_piece(k, c):
            target = base + lax.rem(k + own, heads)

            @pl.when(target != own)
            def _():
                remote(osend.at[target], orecv.at[own], o_send, o_recv, ctx=requests * target + r).start()
                remote(lsend.at[target], lrecv.at[own], l_send, l_recv, ctx=requests * target + r).start()

            return c

        lax.fori_loop(0, heads, send_piece, 0)

    def send_page(k, c):
        peer = lax.rem(me + k, members)

        @pl.when(peer != partner)
        def _():
            remote(kvall.at[me], kvall.at[me], page_send, page_recv, ctx=peer).start()

        return c

    lax.fori_loop(1, members, send_page, 0)

    orecv[own] = osend[own]
    lrecv[own] = lsend[own]
    landed(lrecv.at[pl.ds(0, owners - 1)], l_recv)
    levels = lrecv[...].reshape(owners, HD)
    levels = jnp.concatenate([levels, jnp.full((HD - owners, HD), FLOOR, jnp.float32)], axis=0)
    levels = levels.T[:chunk]
    share = jnp.exp2(levels - jnp.max(levels, axis=1, keepdims=True))
    share = share / jnp.sum(share, axis=1, keepdims=True)
    landed(orecv.at[pl.ds(0, owners - 1)], o_recv)
    done = jnp.zeros((chunk, HD), jnp.float32)
    for s in range(owners):
        done = done + share[:, s : s + 1] * orecv[s].astype(jnp.float32)
    place = abuf.at[lax.rem(own, heads), pl.ds(pl.multiple_of((1 - side) * chunk, chunk), chunk)]
    place[...] = done.astype(abuf.dtype)

    def send_finished(k, c):
        remote(place, place, f_send, f_recv, ctx=lax.rem(me + requests * k, members)).start()
        return c

    lax.fori_loop(1, owners, send_finished, 0)

    landed(kvall.at[pl.ds(0, members - 2)], page_recv)
    for s in range(requests):
        source = jnp.int32(0)
        for b in range(members):
            source = jnp.maximum(source, jnp.where(owner_ref[s, b] == me, b, 0))
        sk_ref[s] = kvall[source, 0, s]
        sv_ref[s] = kvall[source, 1, s]
    load_w.wait()
    give_w.wait_recv()

    flat = abuf.reshape(owners, chunk, HD)
    landed(flat.at[pl.ds(0, owners - 1)], f_recv)
    rows_in = jnp.concatenate([abuf[h] for h in range(heads)], axis=1)
    for j in range(requests):
        part = jnp.dot(rows_in, wbuf[j], preferred_element_type=jnp.float32).astype(psend.dtype)
        for g in range(groups):
            psend[g, j] = part[g * share_rows : (g + 1) * share_rows]

    def send_part(k, c):
        peer = lax.rem(mine + k, groups)
        for j in range(requests):
            remote(psend.at[peer, j], precv.at[mine, r], p_send, p_recv, ctx=me - r + j, tp=peer).start()
        return c

    lax.fori_loop(1, groups, send_part, 0)
    remote(psend.at[mine, other], precv.at[mine, r], p_send, p_recv, ctx=partner).start()
    precv[mine, r] = psend[mine, r]
    flat_parts = precv.reshape(requests * groups, share_rows, precv.shape[3])
    landed(flat_parts.at[pl.ds(0, requests * groups - 1)], p_recv)
    full = precv[0].astype(jnp.float32)
    for g in range(1, groups):
        full = full + precv[g].astype(jnp.float32)
    out_ref[...] = full

    for give in (give_k, give_v, give_w, give_page):
        give.wait_send()
    landed(qall.at[pl.ds(0, members - 1)], q_send)
    landed(kvall.at[pl.ds(0, members - 2)], page_send)
    landed(orecv.at[pl.ds(0, owners - 1)], o_send)
    landed(lrecv.at[pl.ds(0, owners - 1)], l_send)
    landed(flat.at[pl.ds(0, owners - 1)], f_send)
    landed(flat_parts.at[pl.ds(0, requests * groups - 1)], p_send)


def on_device(queries, new_keys, new_values, cache_keys, cache_values, hist_len, page_owner, out_weight):
    members = lax.axis_size("ctx")
    groups = lax.axis_size("tp")
    page, requests, width = queries.shape
    history = cache_keys.shape[1]
    heads = width // HD
    turn = page * members
    chunk = turn // 2
    owners = members // requests
    share_rows = turn // groups
    columns = out_weight.shape[1]
    vmem = pl.BlockSpec(memory_space=pltpu.VMEM)
    smem = pl.BlockSpec(memory_space=pltpu.SMEM)
    anywhere = pl.BlockSpec(memory_space=pl.ANY)
    bf16, f32 = jnp.bfloat16, jnp.float32
    dma = pltpu.SemaphoreType.DMA
    full, kept_keys, kept_values = pl.pallas_call(
        functools.partial(kernel, members, groups),
        out_shape=(
            jax.ShapeDtypeStruct((requests, share_rows, columns), f32),
            jax.ShapeDtypeStruct(new_keys.shape, bf16),
            jax.ShapeDtypeStruct(new_keys.shape, bf16),
        ),
        in_specs=[vmem, vmem, vmem, anywhere, anywhere, smem, smem, anywhere],
        out_specs=[vmem, vmem, vmem],
        scratch_shapes=[
            pltpu.VMEM((2 * history + HD, HD), bf16),
            pltpu.VMEM((2 * history + HD, HD), bf16),
            pltpu.VMEM((requests, *out_weight.shape), bf16),
            pltpu.VMEM((requests, page * heads, HD), f32),
            pltpu.VMEM((HD, HD), f32),
            pltpu.VMEM((requests, page * heads, HD), bf16),
            pltpu.VMEM((members, page * heads, HD), bf16),
            pltpu.VMEM((members, 2, *new_keys.shape), bf16),
            pltpu.VMEM((chunk * heads, 2 * history), f32),
            pltpu.VMEM((chunk * heads, 2 * HD), f32),
            pltpu.VMEM((chunk * heads, HD), f32),
            pltpu.VMEM((chunk * heads, HD), f32),
            pltpu.VMEM((owners, chunk, HD), bf16),
            pltpu.VMEM((owners, 1, HD), f32),
            pltpu.VMEM((owners, chunk, HD), bf16),
            pltpu.VMEM((owners, 1, HD), f32),
            pltpu.VMEM((heads, turn, HD), bf16),
            pltpu.VMEM((groups, requests, share_rows, columns), bf16),
            pltpu.VMEM((groups, requests, share_rows, columns), bf16),
            dma((3,)),
            dma((4,)),
            dma((4,)),
            dma(()),
            dma((2,)),
            dma(()),
            dma(()),
            dma(()),
            dma(()),
            dma(()),
            dma(()),
            dma(()),
            dma(()),
            dma(()),
            dma(()),
        ],
        compiler_params=pltpu.CompilerParams(collective_id=0, has_side_effects=True),
    )(queries, new_keys, new_values, cache_keys, cache_values, hist_len, page_owner, out_weight)
    attended = full.astype(bf16).transpose(1, 0, 2)
    return (attended, kept_keys[None], kept_values[None])


def solution(mesh):
    return jax.shard_map(
        on_device,
        mesh=mesh,
        in_specs=(
            P("ctx", None, "tp"),
            P(None, "ctx", "tp"),
            P(None, "ctx", "tp"),
            P(None, "ctx", "tp"),
            P(None, "ctx", "tp"),
            P(),
            P(),
            P("tp", "ctx"),
        ),
        out_specs=(P("tp", None, "ctx"), P("ctx", None, None, "tp"), P("ctx", None, None, "tp")),
        check_vma=False,
    )
```

time: 59.4 us -> 49.1 us (0.83)
  Pallas kernels: 54.6 us -> 44.5 us
    pallas_call x1, Pallas kernels: 54.6 us -> 44.5 us  [on_device(): pl.pallas_call(functools.partial(kernel, members, groups), out_shape=(jax...]
    reshape x1 -> x0, other arithmetic: 0.72 us -> none  [on_device(): full.astype(bf16).reshape(requests, turn // groups, columns)]
    transpose x0 -> x1, other arithmetic: none -> 0.72 us  [on_device(): attended = full.astype(bf16).transpose(1, 0, 2)]
    reshape x1 -> x0, local copies, waits for them, and re-layouts: 0.61 us -> none  [on_device(): full.astype(bf16).reshape(requests, turn // groups, columns)]
    unnamed x2 -> x3, local copies, waits for them, and re-layouts: 2.45 us -> 3.05 us
where the time goes in v2:
time: 49.1 us; the launch traced here: 48.9 us
  Pallas kernels  44.5 us (91%)
  local copies, waits for them, and re-layouts  3.05 us (6%)
  other arithmetic  0.72 us (1%)
  between operations  0.64 us (1%)
    pallas_call x1, Pallas kernels, on_device(): pl.pallas_call(functools.partial(kernel, members, groups), out_shape=(jax...  44.5 us
    unnamed x3, local copies, waits for them, and re-layouts  3.05 us

profile of v2, /device:TPU:1, one launch (start us, length us, event | category | flops | bytes accessed | tf_op | source)
XLA Modules:
  0.0 48.9 jit_solution(16523240026998039747)
XLA Ops:
  0.6 44.5 %shard_map.103 = (f32[2,8,256]{2,1,0:T(8,128)}, bf16[2,2,128]{2,1,0:T(2,128)(2,1)}, bf16[2,2,128]{2,1,0:T(2,128)(2,1)}) custom-call(bf16[2,2,1024]{2,1,0:T(2,128)(2,1)} %q_ref.1, bf16[2,2,128]{2,1,0:T(2,128)(2,1)} %nk_ref.1, bf16[2,2,128]{2,1,0:T(2,128)(2,1)} %nv_ref.1, bf16[2,4096,128]{2,1,0:T(8,128)(2,1)} %ck_ref.1, bf16[2,4096,128]{2,1,0:T(8,128)(2,1)} %cv_ref.1, ...), custom_call_target="tpu_custom_call" | custom-call | tf_op jit(solution)/shard_map/pallas_call | solution.py:330
  45.1 0.7 %convert_bitcast_fusion = bf16[8,2,256]{2,0,1:T(8,128)(2,1)S(1)} fusion(f32[2,8,256]{2,1,0:T(8,128)} %get-tuple-element.6), kind=kLoop, calls=%fused_computation | loop fusion | flops 4096 | bytes 24576 | tf_op jit(solution)/shard_map/transpose | solution.py:377
  45.8 0.6 %copy.11 = bf16[8,2,256]{2,1,0:T(2,128)(2,1)} copy(bf16[8,2,256]{2,0,1:T(8,128)(2,1)S(1)} %convert_bitcast_fusion) | data formatting | bytes 16384
  46.5 1.2 %copy.14 = bf16[1,2,2,128]{3,2,1,0:T(2,128)(2,1)} copy(bf16[1,2,2,128]{3,2,1,0:T(2,128)(2,1)} %bitcast.5) | data formatting | bytes 2048
  47.7 1.2 %copy.15 = bf16[1,2,2,128]{3,2,1,0:T(2,128)(2,1)} copy(bf16[1,2,2,128]{3,2,1,0:T(2,128)(2,1)} %bitcast.4) | data formatting | bytes 2048

commit v3 on v2

--- a/solution.py
+++ b/solution.py
@@ -10,6 +10,7 @@
 
 HD = 128
 FLOOR = -1e30
+KEY_BLOCK = 4096
 MESH = pl.DeviceIdType.MESH
 
 
@@ -25,14 +26,12 @@
     owner_ref,
     w_ref,
     out_ref,
-    sk_ref,
-    sv_ref,
+    pages_ref,
     kbuf,
     vbuf,
     wbuf,
     qtmp,
     ktail,
-    qown,
     qall,
     kvall,
     scores,
@@ -49,6 +48,8 @@
     load_sem,
     chip_send,
     chip_recv,
+    z_send,
+    z_recv,
     q_send,
     q_recv,
     page_send,
@@ -80,6 +81,10 @@
     r = lax.rem(me, 2)
     other = 1 - r
     partner = me + 1 - 2 * r
+    cell_size = 4
+    depth = members // cell_size
+    across = me + 2 - 4 * lax.rem(me // 2, 2)
+    diagonal = across + 1 - 2 * r
     own = me // 2
     side = own // heads
 
@@ -95,8 +100,8 @@
     def greet(**device):
         pl.semaphore_signal(barrier, inc=1, device_id=device, device_id_type=MESH)
 
-    def greet_ctx(k, c):
-        greet(ctx=lax.rem(me + k, members))
+    def greet_z(k, c):
+        greet(ctx=lax.rem(me + cell_size * k, members))
         return c
 
     def greet_tp(k, c):
@@ -104,7 +109,9 @@
             greet(ctx=me - r + j, tp=lax.rem(mine + k, groups))
         return c
 
-    lax.fori_loop(1, members, greet_ctx, 0)
+    lax.fori_loop(1, depth, greet_z, 0)
+    for cell in (partner, across, diagonal):
+        greet(ctx=cell)
     lax.fori_loop(1, groups, greet_tp, 0)
 
     for t in range(page):
@@ -112,11 +119,11 @@
         for h in range(heads):
             for s in range(requests):
                 qtmp[s, pl.ds(t * heads + h, 1), :] = row[s : s + 1, h * HD : (h + 1) * HD]
-    qown[...] = qtmp[...].astype(qown.dtype)
-    qall[me] = qown[r]
+    qall[me, 0] = qtmp[r].astype(qall.dtype)
+    qall[me, 1] = qtmp[other].astype(qall.dtype)
     kvall[me, 0] = nk_ref[...]
     kvall[me, 1] = nv_ref[...]
-    pl.semaphore_wait(barrier, members - 1 + requests * (groups - 1))
+    pl.semaphore_wait(barrier, depth - 1 + cell_size - 1 + requests * (groups - 1))
 
     def remote(src, dst, send_sem, recv_sem, **device):
         return pltpu.make_async_remote_copy(
@@ -126,19 +133,25 @@
     def landed(ref, sem):
         pltpu.make_async_copy(ref, ref, sem).wait()
 
-    def send_query(peer, where):
-        remote(qown.at[lax.rem(peer, 2)], qall.at[me], q_send, q_recv.at[where], ctx=peer).start()
-
-    def near_query(k, c):
-        send_query(side * near + lax.rem(lax.rem(me, near) + k, near), 0)
-        return c
-
-    def far_query(k, c):
-        send_query((1 - side) * near + lax.rem(lax.rem(me, near) + k, near), 1)
-        return c
-
-    lax.fori_loop(1, near, near_query, 0)
-    lax.fori_loop(0, near, far_query, 0)
+    def by_distance(k):
+        step = (k + 1) // 2
+        return lax.rem(k, 2) * step + (1 - lax.rem(k, 2)) * (depth - step)
+
+    def query_to(peer, source):
+        return remote(qall.at[source], qall.at[source], z_send, z_recv.at[source // cell_size], ctx=peer)
+
+    def send_query(k, c):
+        query_to(lax.rem(me + cell_size * by_distance(depth - k), members), me).start()
+        return c
+
+    lax.fori_loop(1, depth, send_query, 0)
+
+    def pass_on(source):
+        where = q_recv.at[(source // near + side) % 2]
+        for part, target in ((0, across), (1, diagonal), (1, partner)):
+            remote(qall.at[source, part], qall.at[source, 0], q_send, where, ctx=target).start()
+
+    pass_on(me)
 
     history_slab = pl.ds(history, history)
     give_k = remote(ck_ref.at[other], kbuf.at[history_slab], chip_send.at[0], chip_recv.at[0], ctx=partner)
@@ -148,6 +161,14 @@
     give_page.start()
     give_k.start()
     give_v.start()
+
+    def relay(k, c):
+        source = lax.rem(me + cell_size * by_distance(k), members)
+        query_to(me, source).wait_recv()
+        pass_on(source)
+        return c
+
+    lax.fori_loop(1, depth, relay, 0)
     give_w.start()
 
     give_page.wait_recv()
@@ -157,14 +178,15 @@
             ktail[pl.ds(j * page, page), :] = kvall[me - r + j, source, r].astype(jnp.float32)
         target[pl.ds(2 * history, tail), :] = ktail[...].astype(target.dtype)
 
-    ones = jnp.ones((history, HD), jnp.bfloat16)
+    ones = jnp.ones((KEY_BLOCK, HD), jnp.bfloat16)
     row_token = lax.broadcasted_iota(jnp.int32, (rows, tail), 0) // heads
     tail_lane = lax.broadcasted_iota(jnp.int32, (rows, tail), 1)
     token_row = lax.broadcasted_iota(jnp.int32, (chunk, HD), 0)
     token_lane = lax.broadcasted_iota(jnp.int32, (chunk, HD), 1)
-    slot = lax.broadcasted_iota(jnp.int32, (1, history), 1)
-
-    def bias_of(device):
+    lane = lax.broadcasted_iota(jnp.int32, (1, KEY_BLOCK), 1)
+
+    def bias_of(device, offset):
+        slot = lane + offset
         low = hist_ref[r] - device * half_size
         high = hist_ref[r] - (2 * members - 1 - device) * half_size + half_size
         return jnp.where(slot < jnp.where(slot < half_size, low, high), 0.0, FLOOR)
@@ -175,44 +197,56 @@
         preferred_element_type=jnp.float32,
     )
 
-    def score(queries, b, device, peak):
-        block = dot_nt(queries, kbuf[b * history : (b + 1) * history, :]) + bias_of(device)
-        scores[:, b * history : (b + 1) * history] = block
-        for p in range(history // HD):
-            peak = jnp.maximum(peak, block[:, p * HD : (p + 1) * HD])
-        return peak
-
-    def weigh(b, peak):
-        weights = jnp.exp2((scores[:, b * history : (b + 1) * history] - peak) * factor).astype(jnp.bfloat16)
-        values = jnp.concatenate([vbuf[b * history : (b + 1) * history, :], ones], axis=1)
-        return jnp.dot(weights, values, preferred_element_type=jnp.float32)
-
-    for turn_half in range(2):
-        which = side if turn_half == 0 else 1 - side
+    steps = 2 * history // KEY_BLOCK
+    relayed = qall.at[pl.ds(0, near - near // cell_size), 0]
+
+    def attend(i, c):
+        which = lax.rem(side + i, 2)
         first = which * near
-        if turn_half == 0:
-            landed(qall.at[pl.ds(0, near - 1)], q_recv.at[0])
+
+        @pl.when(i == 0)
+        def _():
             load_k.wait()
-        else:
-            landed(qall.at[pl.ds(0, near)], q_recv.at[1])
-        queries = qall[pl.ds(first, near)].reshape(rows, HD)
+
+        landed(relayed, q_recv.at[i])
+        queries = qall[pl.ds(first, near), 0].reshape(rows, HD)
+
+        def score(b, peak):
+            offset = pl.multiple_of(b * KEY_BLOCK, KEY_BLOCK)
+
+            @pl.when((i == 0) & (offset == history))
+            def _():
+                give_k.wait_recv()
+
+            given = offset // history
+            block = dot_nt(queries, kbuf[pl.ds(offset, KEY_BLOCK), :])
+            block = block + bias_of(me + (partner - me) * given, offset - history * given)
+            scores[:, pl.ds(offset, KEY_BLOCK)] = block
+            for p in range(KEY_BLOCK // HD):
+                peak = jnp.maximum(peak, block[:, p * HD : (p + 1) * HD])
+            return peak
+
         last = dot_nt(queries, kbuf[2 * history :, :])
         visible = (tail_lane < 2 * page) & (tail_lane + 2 * page * own <= row_token + which * chunk)
         last = jnp.where(visible, last, FLOOR)
-        peak = score(queries, 0, me, last)
-        if turn_half == 0:
-            give_k.wait_recv()
-        peak = score(queries, 1, partner, peak)
-        peak = jnp.max(peak, axis=1, keepdims=True)
+        peak = jnp.max(lax.fori_loop(0, steps, score, last), axis=1, keepdims=True)
         weights = jnp.exp2((last - peak) * factor).astype(jnp.bfloat16)
         values = jnp.concatenate([vbuf[2 * history :, :], ones[:tail]], axis=1)
         acc[...] = jnp.dot(weights, values, preferred_element_type=jnp.float32)
-        if turn_half == 0:
+
+        @pl.when(i == 0)
+        def _():
             load_v.wait()
-        acc[...] += weigh(0, peak)
-        if turn_half == 0:
             give_v.wait_recv()
-        acc[...] += weigh(1, peak)
+
+        def weigh(b, c):
+            offset = pl.multiple_of(b * KEY_BLOCK, KEY_BLOCK)
+            weights = jnp.exp2((scores[:, pl.ds(offset, KEY_BLOCK)] - peak) * factor).astype(jnp.bfloat16)
+            values = jnp.concatenate([vbuf[pl.ds(offset, KEY_BLOCK), :], ones], axis=1)
+            acc[...] += jnp.dot(weights, values, preferred_element_type=jnp.float32)
+            return c
+
+        lax.fori_loop(0, steps, weigh, 0)
         total = acc[:, HD:]
         lse[...] = peak * factor + jnp.log2(total)
         ready[...] = acc[:, :HD] / total
@@ -234,6 +268,9 @@
             return c
 
         lax.fori_loop(0, heads, send_piece, 0)
+        return c
+
+    lax.fori_loop(0, 2, attend, 0)
 
     def send_page(k, c):
         peer = lax.rem(me + k, members)
@@ -272,8 +309,8 @@
         source = jnp.int32(0)
         for b in range(members):
             source = jnp.maximum(source, jnp.where(owner_ref[s, b] == me, b, 0))
-        sk_ref[s] = kvall[source, 0, s]
-        sv_ref[s] = kvall[source, 1, s]
+        for kind in range(2):
+            pages_ref[kind, s] = kvall[source, kind, s]
     load_w.wait()
     give_w.wait_recv()
 
@@ -303,12 +340,21 @@
 
     for give in (give_k, give_v, give_w, give_page):
         give.wait_send()
-    landed(qall.at[pl.ds(0, members - 1)], q_send)
+    landed(qall.at[pl.ds(0, depth - 1)], z_send)
+    for _ in range(2):
+        landed(relayed, q_send)
     landed(kvall.at[pl.ds(0, members - 2)], page_send)
     landed(orecv.at[pl.ds(0, owners - 1)], o_send)
     landed(lrecv.at[pl.ds(0, owners - 1)], l_send)
     landed(flat.at[pl.ds(0, owners - 1)], f_send)
     landed(flat_parts.at[pl.ds(0, requests * groups - 1)], p_send)
+
+
+def finish(full_ref, pages_ref, attended_ref, keys_ref, values_ref):
+    parts = [full_ref[r] for r in range(full_ref.shape[0])]
+    attended_ref[...] = jnp.stack(parts, axis=1).astype(attended_ref.dtype)
+    keys_ref[0] = pages_ref[0]
+    values_ref[0] = pages_ref[1]
 
 
 def on_device(queries, new_keys, new_values, cache_keys, cache_values, hist_len, page_owner, out_weight):
@@ -327,23 +373,21 @@
     anywhere = pl.BlockSpec(memory_space=pl.ANY)
     bf16, f32 = jnp.bfloat16, jnp.float32
     dma = pltpu.SemaphoreType.DMA
-    full, kept_keys, kept_values = pl.pallas_call(
+    full, pages = pl.pallas_call(
         functools.partial(kernel, members, groups),
         out_shape=(
             jax.ShapeDtypeStruct((requests, share_rows, columns), f32),
-            jax.ShapeDtypeStruct(new_keys.shape, bf16),
-            jax.ShapeDtypeStruct(new_keys.shape, bf16),
+            jax.ShapeDtypeStruct((2, *new_keys.shape), bf16),
         ),
         in_specs=[vmem, vmem, vmem, anywhere, anywhere, smem, smem, anywhere],
-        out_specs=[vmem, vmem, vmem],
+        out_specs=[vmem, vmem],
         scratch_shapes=[
             pltpu.VMEM((2 * history + HD, HD), bf16),
             pltpu.VMEM((2 * history + HD, HD), bf16),
             pltpu.VMEM((requests, *out_weight.shape), bf16),
             pltpu.VMEM((requests, page * heads, HD), f32),
             pltpu.VMEM((HD, HD), f32),
-            pltpu.VMEM((requests, page * heads, HD), bf16),
-            pltpu.VMEM((members, page * heads, HD), bf16),
+            pltpu.VMEM((members, requests, page * heads, HD), bf16),
             pltpu.VMEM((members, 2, *new_keys.shape), bf16),
             pltpu.VMEM((chunk * heads, 2 * history), f32),
             pltpu.VMEM((chunk * heads, 2 * HD), f32),
@@ -360,6 +404,8 @@
             dma((4,)),
             dma((4,)),
             dma(()),
+            dma((members // 4,)),
+            dma(()),
             dma((2,)),
             dma(()),
             dma(()),
@@ -374,8 +420,13 @@
         ],
         compiler_params=pltpu.CompilerParams(collective_id=0, has_side_effects=True),
     )(queries, new_keys, new_values, cache_keys, cache_values, hist_len, page_owner, out_weight)
-    attended = full.astype(bf16).transpose(1, 0, 2)
-    return (attended, kept_keys[None], kept_values[None])
+    pages_shape = jax.ShapeDtypeStruct((1, *new_keys.shape), bf16)
+    return pl.pallas_call(
+        finish,
+        out_shape=(jax.ShapeDtypeStruct((share_rows, requests, columns), bf16), pages_shape, pages_shape),
+        in_specs=[vmem, vmem],
+        out_specs=[vmem, vmem, vmem],
+    )(full, pages)
 
 
 def solution(mesh):

time: 49.1 us -> 45.6 us (0.929)
  local copies, waits for them, and re-layouts: 3.05 us -> 0 us
  other arithmetic: 0.72 us -> 0 us
    unnamed x3 -> x0, local copies, waits for them, and re-layouts: 3.05 us -> none
    pallas_call x0 -> x1, Pallas kernels: none -> 1.34 us  [on_device(): pl.pallas_call(finish, out_shape=(jax.ShapeDtypeStruct((share_rows, reque...]
    pallas_call x1, Pallas kernels: 44.5 us -> 43.4 us  [on_device(): pl.pallas_call(functools.partial(kernel, members, groups), out_shape=(jax...]
    transpose x1 -> x0, other arithmetic: 0.72 us -> none  [on_device(): attended = full.astype(bf16).transpose(1, 0, 2)]
where the time goes in v3:
time: 45.6 us; the launch traced here: 45.4 us
  Pallas kernels  44.8 us (98%)
  between operations  0.64 us (1%)
    pallas_call x1, Pallas kernels, on_device(): pl.pallas_call(functools.partial(kernel, members, groups), out_shape=(jax...  43.4 us
    pallas_call x1, Pallas kernels, on_device(): pl.pallas_call(finish, out_shape=(jax.ShapeDtypeStruct((share_rows, reque...  1.34 us

profile of v3, /device:TPU:1, one launch (start us, length us, event | category | flops | bytes accessed | tf_op | source)
XLA Modules:
  0.0 45.4 jit_solution(17675558127009172771)
XLA Ops:
  0.6 43.4 %shard_map.103 = (f32[2,8,256]{2,1,0:T(8,128)}, bf16[2,2,2,128]{3,2,1,0:T(2,128)(2,1)}) custom-call(bf16[2,2,1024]{2,1,0:T(2,128)(2,1)} %q_ref.1, bf16[2,2,128]{2,1,0:T(2,128)(2,1)} %nk_ref.1, bf16[2,2,128]{2,1,0:T(2,128)(2,1)} %nv_ref.1, bf16[2,4096,128]{2,1,0:T(8,128)(2,1)} %ck_ref.1, bf16[2,4096,128]{2,1,0:T(8,128)(2,1)} %cv_ref.1, s32[2]{0:T(128)} %hist_ref.1, ...), custom_call_target="tpu_custom_call" | custom-call | tf_op jit(solution)/shard_map/pallas_call | solution.py:376
  44.1 1.3 %shard_map.104 = (bf16[8,2,256]{2,1,0:T(2,128)(2,1)}, bf16[1,2,2,128]{3,2,1,0:T(2,128)(2,1)}, bf16[1,2,2,128]{3,2,1,0:T(2,128)(2,1)}) custom-call(f32[2,8,256]{2,1,0:T(8,128)} %get-tuple-element.5.full_ref, bf16[2,2,2,128]{3,2,1,0:T(2,128)(2,1)} %get-tuple-element.6.pages_ref), custom_call_target="tpu_custom_call" | custom-call | tf_op jit(solution)/shard_map/pallas_call | solution.py:424

commit v4 on v3

--- a/solution.py
+++ b/solution.py
@@ -74,6 +74,7 @@
     half_size = history // 2
     owners = members // requests
     near = members // 2
+    quarter = turn // groups // 2
     share_rows = turn // groups
     tail = kbuf.shape[0] - 2 * history
     factor = math.log2(math.e) / math.sqrt(HD)
@@ -86,7 +87,8 @@
     across = me + 2 - 4 * lax.rem(me // 2, 2)
     diagonal = across + 1 - 2 * r
     own = me // 2
-    side = own // heads
+    side = lax.rem(own, 2)
+    level = own // 2
 
     load_k = pltpu.make_async_copy(ck_ref.at[r], kbuf.at[pl.ds(0, history)], load_sem.at[0])
     load_v = pltpu.make_async_copy(cv_ref.at[r], vbuf.at[pl.ds(0, history)], load_sem.at[1])
@@ -119,8 +121,11 @@
         for h in range(heads):
             for s in range(requests):
                 qtmp[s, pl.ds(t * heads + h, 1), :] = row[s : s + 1, h * HD : (h + 1) * HD]
-    qall[me, 0] = qtmp[r].astype(qall.dtype)
-    qall[me, 1] = qtmp[other].astype(qall.dtype)
+    def slot_of(device):
+        return lax.rem(device // 2, 2) * near + device // 4 * 2 + lax.rem(device, 2)
+
+    qall[slot_of(me), 0] = qtmp[r].astype(qall.dtype)
+    qall[slot_of(me), 1] = qtmp[other].astype(qall.dtype)
     kvall[me, 0] = nk_ref[...]
     kvall[me, 1] = nv_ref[...]
     pl.semaphore_wait(barrier, depth - 1 + cell_size - 1 + requests * (groups - 1))
@@ -138,7 +143,8 @@
         return lax.rem(k, 2) * step + (1 - lax.rem(k, 2)) * (depth - step)
 
     def query_to(peer, source):
-        return remote(qall.at[source], qall.at[source], z_send, z_recv.at[source // cell_size], ctx=peer)
+        block = qall.at[slot_of(source)]
+        return remote(block, block, z_send, z_recv.at[source // cell_size], ctx=peer)
 
     def send_query(k, c):
         query_to(lax.rem(me + cell_size * by_distance(depth - k), members), me).start()
@@ -147,9 +153,9 @@
     lax.fori_loop(1, depth, send_query, 0)
 
     def pass_on(source):
-        where = q_recv.at[(source // near + side) % 2]
-        for part, target in ((0, across), (1, diagonal), (1, partner)):
-            remote(qall.at[source, part], qall.at[source, 0], q_send, where, ctx=target).start()
+        slot = slot_of(source)
+        for part, target, chunk_id in ((0, across, 1), (1, diagonal, 1), (1, partner, 0)):
+            remote(qall.at[slot, part], qall.at[slot, 0], q_send, q_recv.at[chunk_id], ctx=target).start()
 
     pass_on(me)
 
@@ -179,7 +185,8 @@
         target[pl.ds(2 * history, tail), :] = ktail[...].astype(target.dtype)
 
     ones = jnp.ones((KEY_BLOCK, HD), jnp.bfloat16)
-    row_token = lax.broadcasted_iota(jnp.int32, (rows, tail), 0) // heads
+    row_index = lax.broadcasted_iota(jnp.int32, (rows, tail), 0) // heads
+    row_token = row_index // quarter * (2 * quarter) + lax.rem(row_index, quarter)
     tail_lane = lax.broadcasted_iota(jnp.int32, (rows, tail), 1)
     token_row = lax.broadcasted_iota(jnp.int32, (chunk, HD), 0)
     token_lane = lax.broadcasted_iota(jnp.int32, (chunk, HD), 1)
@@ -198,7 +205,6 @@
     )
 
     steps = 2 * history // KEY_BLOCK
-    relayed = qall.at[pl.ds(0, near - near // cell_size), 0]
 
     def attend(i, c):
         which = lax.rem(side + i, 2)
@@ -207,8 +213,12 @@
         @pl.when(i == 0)
         def _():
             load_k.wait()
-
-        landed(relayed, q_recv.at[i])
+            landed(qall.at[pl.ds(0, depth), 0], q_recv.at[0])
+
+        @pl.when(i == 1)
+        def _():
+            landed(qall.at[pl.ds(0, near), 0], q_recv.at[1])
+
         queries = qall[pl.ds(first, near), 0].reshape(rows, HD)
 
         def score(b, peak):
@@ -227,7 +237,7 @@
             return peak
 
         last = dot_nt(queries, kbuf[2 * history :, :])
-        visible = (tail_lane < 2 * page) & (tail_lane + 2 * page * own <= row_token + which * chunk)
+        visible = (tail_lane < 2 * page) & (tail_lane + 2 * page * own <= row_token + which * quarter)
         last = jnp.where(visible, last, FLOOR)
         peak = jnp.max(lax.fori_loop(0, steps, score, last), axis=1, keepdims=True)
         weights = jnp.exp2((last - peak) * factor).astype(jnp.bfloat16)
@@ -251,14 +261,13 @@
         lse[...] = peak * factor + jnp.log2(total)
         ready[...] = acc[:, :HD] / total
 
-        base = (1 - which) * heads
         for h in range(heads):
             picked = pl.ds(h, chunk, stride=heads)
-            osend[base + h] = ready[picked, :].astype(osend.dtype)
-            lsend[base + h] = jnp.sum(jnp.where(token_row == token_lane, lse[picked, :], 0.0), axis=0, keepdims=True)
+            osend[2 * h + 1 - which] = ready[picked, :].astype(osend.dtype)
+            lsend[2 * h + 1 - which] = jnp.sum(jnp.where(token_row == token_lane, lse[picked, :], 0.0), axis=0, keepdims=True)
 
         def send_piece(k, c):
-            target = base + lax.rem(k + own, heads)
+            target = 2 * lax.rem(k + level, heads) + 1 - which
 
             @pl.when(target != own)
             def _():
@@ -295,7 +304,7 @@
     done = jnp.zeros((chunk, HD), jnp.float32)
     for s in range(owners):
         done = done + share[:, s : s + 1] * orecv[s].astype(jnp.float32)
-    place = abuf.at[lax.rem(own, heads), pl.ds(pl.multiple_of((1 - side) * chunk, chunk), chunk)]
+    place = abuf.at[level, pl.ds(pl.multiple_of((1 - side) * chunk, chunk), chunk)]
     place[...] = done.astype(abuf.dtype)
 
     def send_finished(k, c):
@@ -318,9 +327,10 @@
     landed(flat.at[pl.ds(0, owners - 1)], f_recv)
     rows_in = jnp.concatenate([abuf[h] for h in range(heads)], axis=1)
     for j in range(requests):
-        part = jnp.dot(rows_in, wbuf[j], preferred_element_type=jnp.float32).astype(psend.dtype)
+        part = jnp.dot(rows_in, wbuf[j], preferred_element_type=jnp.float32)
         for g in range(groups):
-            psend[g, j] = part[g * share_rows : (g + 1) * share_rows]
+            halves = [part[y * chunk + g * quarter : y * chunk + (g + 1) * quarter] for y in range(2)]
+            psend[g, j] = jnp.concatenate(halves, axis=0).astype(psend.dtype)
 
     def send_part(k, c):
         peer = lax.rem(mine + k, groups)
@@ -341,8 +351,7 @@
     for give in (give_k, give_v, give_w, give_page):
         give.wait_send()
     landed(qall.at[pl.ds(0, depth - 1)], z_send)
-    for _ in range(2):
-        landed(relayed, q_send)
+    landed(qall.at[pl.ds(0, 3 * depth), 0], q_send)
     landed(kvall.at[pl.ds(0, members - 2)], page_send)
     landed(orecv.at[pl.ds(0, owners - 1)], o_send)
     landed(lrecv.at[pl.ds(0, owners - 1)], l_send)

time: 45.6 us -> 42.4 us (0.930)
  Pallas kernels: 44.8 us -> 41.5 us
    pallas_call x1, Pallas kernels: 43.4 us -> 40.2 us  [on_device(): pl.pallas_call(functools.partial(kernel, members, groups), out_shape=(jax...]
where the time goes in v4:
time: 42.4 us; the launch traced here: 42.2 us
  Pallas kernels  41.5 us (98%)
  between operations  0.64 us (2%)
    pallas_call x1, Pallas kernels, on_device(): pl.pallas_call(functools.partial(kernel, members, groups), out_shape=(jax...  40.2 us
    pallas_call x1, Pallas kernels, on_device(): pl.pallas_call(finish, out_shape=(jax.ShapeDtypeStruct((share_rows, reque...  1.34 us

profile of v4, /device:TPU:1, one launch (start us, length us, event | category | flops | bytes accessed | tf_op | source)
XLA Modules:
  0.0 42.2 jit_solution(12475639031768412124)
XLA Ops:
  0.6 40.2 %shard_map.103 = (f32[2,8,256]{2,1,0:T(8,128)}, bf16[2,2,2,128]{3,2,1,0:T(2,128)(2,1)}) custom-call(bf16[2,2,1024]{2,1,0:T(2,128)(2,1)} %q_ref.1, bf16[2,2,128]{2,1,0:T(2,128)(2,1)} %nk_ref.1, bf16[2,2,128]{2,1,0:T(2,128)(2,1)} %nv_ref.1, bf16[2,4096,128]{2,1,0:T(8,128)(2,1)} %ck_ref.1, bf16[2,4096,128]{2,1,0:T(8,128)(2,1)} %cv_ref.1, s32[2]{0:T(128)} %hist_ref.1, ...), custom_call_target="tpu_custom_call" | custom-call | tf_op jit(solution)/shard_map/pallas_call | solution.py:385
  40.8 1.3 %shard_map.104 = (bf16[8,2,256]{2,1,0:T(2,128)(2,1)}, bf16[1,2,2,128]{3,2,1,0:T(2,128)(2,1)}, bf16[1,2,2,128]{3,2,1,0:T(2,128)(2,1)}) custom-call(f32[2,8,256]{2,1,0:T(8,128)} %get-tuple-element.5.full_ref, bf16[2,2,2,128]{3,2,1,0:T(2,128)(2,1)} %get-tuple-element.6.pages_ref), custom_call_target="tpu_custom_call" | custom-call | tf_op jit(solution)/shard_map/pallas_call | solution.py:433

commit v5 on v4

--- a/solution.py
+++ b/solution.py
@@ -17,16 +17,19 @@
 def kernel(
     members,
     groups,
-    q_ref,
-    nk_ref,
-    nv_ref,
+    q_hbm,
+    nk_hbm,
+    nv_hbm,
     ck_ref,
     cv_ref,
-    hist_ref,
-    owner_ref,
+    hist_hbm,
+    owner_hbm,
     w_ref,
     out_ref,
     pages_ref,
+    q_ref,
+    hist_ref,
+    owner_ref,
     kbuf,
     vbuf,
     wbuf,
@@ -66,8 +69,8 @@
     me = lax.axis_index("ctx")
     mine = lax.axis_index("tp")
     requests, history = ck_ref.shape[:2]
-    page = q_ref.shape[0]
-    heads = q_ref.shape[2] // HD
+    page = q_hbm.shape[0]
+    heads = q_hbm.shape[2] // HD
     turn = page * members
     chunk = turn // 2
     rows = chunk * heads
@@ -93,17 +96,26 @@
     load_k = pltpu.make_async_copy(ck_ref.at[r], kbuf.at[pl.ds(0, history)], load_sem.at[0])
     load_v = pltpu.make_async_copy(cv_ref.at[r], vbuf.at[pl.ds(0, history)], load_sem.at[1])
     load_w = pltpu.make_async_copy(w_ref, wbuf.at[r], load_sem.at[2])
-    load_k.start()
-    load_v.start()
-    load_w.start()
+    load_q = pltpu.make_async_copy(q_hbm, q_ref, load_sem.at[3])
+    load_pages = (
+        pltpu.make_async_copy(nk_hbm, kvall.at[me, 0], load_sem.at[4]),
+        pltpu.make_async_copy(nv_hbm, kvall.at[me, 1], load_sem.at[5]),
+    )
+    load_hist = pltpu.make_async_copy(hist_hbm, hist_ref, load_sem.at[6])
+    load_owner = pltpu.make_async_copy(owner_hbm, owner_ref, load_sem.at[7])
+    load_q.start()
 
     barrier = pltpu.get_barrier_semaphore()
 
     def greet(**device):
         pl.semaphore_signal(barrier, inc=1, device_id=device, device_id_type=MESH)
 
+    def by_distance(k):
+        step = (k + 1) // 2
+        return lax.rem(k, 2) * step + (1 - lax.rem(k, 2)) * (depth - step)
+
     def greet_z(k, c):
-        greet(ctx=lax.rem(me + cell_size * k, members))
+        greet(ctx=lax.rem(me + cell_size * by_distance(depth - k), members))
         return c
 
     def greet_tp(k, c):
@@ -115,6 +127,9 @@
     for cell in (partner, across, diagonal):
         greet(ctx=cell)
     lax.fori_loop(1, groups, greet_tp, 0)
+    for copy in (*load_pages, load_hist, load_owner, load_k, load_v, load_w):
+        copy.start()
+    load_q.wait()
 
     for t in range(page):
         row = q_ref[t].astype(jnp.float32)
@@ -126,8 +141,6 @@
 
     qall[slot_of(me), 0] = qtmp[r].astype(qall.dtype)
     qall[slot_of(me), 1] = qtmp[other].astype(qall.dtype)
-    kvall[me, 0] = nk_ref[...]
-    kvall[me, 1] = nv_ref[...]
     pl.semaphore_wait(barrier, depth - 1 + cell_size - 1 + requests * (groups - 1))
 
     def remote(src, dst, send_sem, recv_sem, **device):
@@ -137,10 +150,6 @@
 
     def landed(ref, sem):
         pltpu.make_async_copy(ref, ref, sem).wait()
-
-    def by_distance(k):
-        step = (k + 1) // 2
-        return lax.rem(k, 2) * step + (1 - lax.rem(k, 2)) * (depth - step)
 
     def query_to(peer, source):
         block = qall.at[slot_of(source)]
@@ -164,6 +173,8 @@
     give_v = remote(cv_ref.at[other], vbuf.at[history_slab], chip_send.at[1], chip_recv.at[1], ctx=partner)
     give_w = remote(w_ref, wbuf.at[r], chip_send.at[2], chip_recv.at[2], ctx=partner)
     give_page = remote(kvall.at[me], kvall.at[me], chip_send.at[3], chip_recv.at[3], ctx=partner)
+    for copy in load_pages:
+        copy.wait()
     give_page.start()
     give_k.start()
     give_v.start()
@@ -261,24 +272,35 @@
         lse[...] = peak * factor + jnp.log2(total)
         ready[...] = acc[:, :HD] / total
 
-        for h in range(heads):
+        def pack(h):
             picked = pl.ds(h, chunk, stride=heads)
-            osend[2 * h + 1 - which] = ready[picked, :].astype(osend.dtype)
-            lsend[2 * h + 1 - which] = jnp.sum(jnp.where(token_row == token_lane, lse[picked, :], 0.0), axis=0, keepdims=True)
-
-        def send_piece(k, c):
-            target = 2 * lax.rem(k + level, heads) + 1 - which
+            target = 2 * h + 1 - which
+            osend[target] = ready[picked, :].astype(osend.dtype)
+            lsend[target] = jnp.sum(jnp.where(token_row == token_lane, lse[picked, :], 0.0), axis=0, keepdims=True)
+
+        def send_piece(h):
+            target = 2 * h + 1 - which
 
             @pl.when(target != own)
             def _():
                 remote(osend.at[target], orecv.at[own], o_send, o_recv, ctx=requests * target + r).start()
                 remote(lsend.at[target], lrecv.at[own], l_send, l_recv, ctx=requests * target + r).start()
 
+        def turned(k):
+            return lax.rem(k + level, heads)
+
+        def piece(k, c):
+            pack(turned(k))
+            send_piece(turned(k - 1))
             return c
 
-        lax.fori_loop(0, heads, send_piece, 0)
-        return c
-
+        pack(turned(0))
+        lax.fori_loop(1, heads, piece, 0)
+        send_piece(turned(heads - 1))
+        return c
+
+    load_hist.wait()
+    load_owner.wait()
     lax.fori_loop(0, 2, attend, 0)
 
     def send_page(k, c):
@@ -326,11 +348,14 @@
     flat = abuf.reshape(owners, chunk, HD)
     landed(flat.at[pl.ds(0, owners - 1)], f_recv)
     rows_in = jnp.concatenate([abuf[h] for h in range(heads)], axis=1)
-    for j in range(requests):
+    def project(j, c):
         part = jnp.dot(rows_in, wbuf[j], preferred_element_type=jnp.float32)
         for g in range(groups):
             halves = [part[y * chunk + g * quarter : y * chunk + (g + 1) * quarter] for y in range(2)]
             psend[g, j] = jnp.concatenate(halves, axis=0).astype(psend.dtype)
+        return c
+
+    lax.fori_loop(0, requests, project, 0)
 
     def send_part(k, c):
         peer = lax.rem(mine + k, groups)
@@ -378,7 +403,6 @@
     share_rows = turn // groups
     columns = out_weight.shape[1]
     vmem = pl.BlockSpec(memory_space=pltpu.VMEM)
-    smem = pl.BlockSpec(memory_space=pltpu.SMEM)
     anywhere = pl.BlockSpec(memory_space=pl.ANY)
     bf16, f32 = jnp.bfloat16, jnp.float32
     dma = pltpu.SemaphoreType.DMA
@@ -388,9 +412,12 @@
             jax.ShapeDtypeStruct((requests, share_rows, columns), f32),
             jax.ShapeDtypeStruct((2, *new_keys.shape), bf16),
         ),
-        in_specs=[vmem, vmem, vmem, anywhere, anywhere, smem, smem, anywhere],
+        in_specs=[anywhere] * 8,
         out_specs=[vmem, vmem],
         scratch_shapes=[
+            pltpu.VMEM(queries.shape, bf16),
+            pltpu.SMEM(hist_len.shape, jnp.int32),
+            pltpu.SMEM(page_owner.shape, jnp.int32),
             pltpu.VMEM((2 * history + HD, HD), bf16),
             pltpu.VMEM((2 * history + HD, HD), bf16),
             pltpu.VMEM((requests, *out_weight.shape), bf16),
@@ -409,7 +436,7 @@
             pltpu.VMEM((heads, turn, HD), bf16),
             pltpu.VMEM((groups, requests, share_rows, columns), bf16),
             pltpu.VMEM((groups, requests, share_rows, columns), bf16),
-            dma((3,)),
+            dma((8,)),
             dma((4,)),
             dma((4,)),
             dma(()),

time: 42.4 us -> 41.8 us (0.986)
  Pallas kernels: 41.5 us -> 40.9 us
    pallas_call x1, Pallas kernels: 40.2 us -> 39.6 us  [on_device(): pl.pallas_call(functools.partial(kernel, members, groups), out_shape=(jax...]
where the time goes in v5:
time: 41.8 us; the launch traced here: 41.5 us
  Pallas kernels  40.9 us (98%)
  between operations  0.64 us (2%)
    pallas_call x1, Pallas kernels, on_device(): pl.pallas_call(functools.partial(kernel, members, groups), out_shape=(jax...  39.6 us
    pallas_call x1, Pallas kernels, on_device(): pl.pallas_call(finish, out_shape=(jax.ShapeDtypeStruct((share_rows, reque...  1.34 us

profile of v5, /device:TPU:1, one launch (start us, length us, event | category | flops | bytes accessed | tf_op | source)
XLA Modules:
  0.0 41.5 jit_solution(417240998262447298)
XLA Ops:
  0.6 39.6 %shard_map.103 = (f32[2,8,256]{2,1,0:T(8,128)}, bf16[2,2,2,128]{3,2,1,0:T(2,128)(2,1)}) custom-call(bf16[2,2,1024]{2,1,0:T(2,128)(2,1)} %q_hbm.1, bf16[2,2,128]{2,1,0:T(2,128)(2,1)} %nk_hbm.1, bf16[2,2,128]{2,1,0:T(2,128)(2,1)} %nv_hbm.1, bf16[2,4096,128]{2,1,0:T(8,128)(2,1)} %ck_ref.1, bf16[2,4096,128]{2,1,0:T(8,128)(2,1)} %cv_ref.1, s32[2]{0:T(128)} %hist_hbm.1, ...), custom_call_target="tpu_custom_call" | custom-call | tf_op jit(solution)/shard_map/pallas_call | solution.py:409
  40.2 1.3 %shard_map.104 = (bf16[8,2,256]{2,1,0:T(2,128)(2,1)}, bf16[1,2,2,128]{3,2,1,0:T(2,128)(2,1)}, bf16[1,2,2,128]{3,2,1,0:T(2,128)(2,1)}) custom-call(f32[2,8,256]{2,1,0:T(8,128)} %get-tuple-element.5.full_ref, bf16[2,2,2,128]{3,2,1,0:T(2,128)(2,1)} %get-tuple-element.6.pages_ref), custom_call_target="tpu_custom_call" | custom-call | tf_op jit(solution)/shard_map/pallas_call | solution.py:460

commit v6 on v5

--- a/solution.py
+++ b/solution.py
@@ -353,17 +353,16 @@
         for g in range(groups):
             halves = [part[y * chunk + g * quarter : y * chunk + (g + 1) * quarter] for y in range(2)]
             psend[g, j] = jnp.concatenate(halves, axis=0).astype(psend.dtype)
+
+        def send_part(k, c):
+            peer = lax.rem(mine + k, groups)
+            remote(psend.at[peer, j], precv.at[mine, r], p_send, p_recv, ctx=me - r + j, tp=peer).start()
+            return c
+
+        lax.fori_loop(1, groups, send_part, 0)
         return c
 
     lax.fori_loop(0, requests, project, 0)
-
-    def send_part(k, c):
-        peer = lax.rem(mine + k, groups)
-        for j in range(requests):
-            remote(psend.at[peer, j], precv.at[mine, r], p_send, p_recv, ctx=me - r + j, tp=peer).start()
-        return c
-
-    lax.fori_loop(1, groups, send_part, 0)
     remote(psend.at[mine, other], precv.at[mine, r], p_send, p_recv, ctx=partner).start()
     precv[mine, r] = psend[mine, r]
     flat_parts = precv.reshape(requests * groups, share_rows, precv.shape[3])

time: 41.8 us -> 41.6 us (level)
  no operation moved by 1% of the time
where the time goes in v6:
time: 41.6 us; the launch traced here: 41.4 us
  Pallas kernels  40.7 us (98%)
  between operations  0.64 us (2%)
    pallas_call x1, Pallas kernels, on_device(): pl.pallas_call(functools.partial(kernel, members, groups), out_shape=(jax...  39.4 us
    pallas_call x1, Pallas kernels, on_device(): pl.pallas_call(finish, out_shape=(jax.ShapeDtypeStruct((share_rows, reque...  1.34 us

profile of v6, /device:TPU:1, one launch (start us, length us, event | category | flops | bytes accessed | tf_op | source)
XLA Modules:
  0.0 41.4 jit_solution(12928681966205225827)
XLA Ops:
  0.6 39.4 %shard_map.103 = (f32[2,8,256]{2,1,0:T(8,128)}, bf16[2,2,2,128]{3,2,1,0:T(2,128)(2,1)}) custom-call(bf16[2,2,1024]{2,1,0:T(2,128)(2,1)} %q_hbm.1, bf16[2,2,128]{2,1,0:T(2,128)(2,1)} %nk_hbm.1, bf16[2,2,128]{2,1,0:T(2,128)(2,1)} %nv_hbm.1, bf16[2,4096,128]{2,1,0:T(8,128)(2,1)} %ck_ref.1, bf16[2,4096,128]{2,1,0:T(8,128)(2,1)} %cv_ref.1, s32[2]{0:T(128)} %hist_hbm.1, ...), custom_call_target="tpu_custom_call" | custom-call | tf_op jit(solution)/shard_map/pallas_call | solution.py:408
  40.0 1.3 %shard_map.104 = (bf16[8,2,256]{2,1,0:T(2,128)(2,1)}, bf16[1,2,2,128]{3,2,1,0:T(2,128)(2,1)}, bf16[1,2,2,128]{3,2,1,0:T(2,128)(2,1)}) custom-call(f32[2,8,256]{2,1,0:T(8,128)} %get-tuple-element.5.full_ref, bf16[2,2,2,128]{3,2,1,0:T(2,128)(2,1)} %get-tuple-element.6.pages_ref), custom_call_target="tpu_custom_call" | custom-call | tf_op jit(solution)/shard_map/pallas_call | solution.py:459
